TPU v7x, 32 devices: a whole 2x2x4 slice. The times are simulated.
32 devices in a mesh: tm: 4 (over y, x), space: 8 (over z, core).
Axes of the slice: x: 2, y: 2, z: 4, core: 2. Of those that a mesh axis runs over, the one named last changes fastest.
Arguments:
- image: float32 [16, 256, 512], P('space', None, 'tm'), may hold values from -6 to 6
- inv_var: float32 [16, 256, 512], P('space', None, 'tm'), may hold values from 0.25 to 4
- psf: float32 [15, 15], replicated, may hold values from 0.001 to 1
- shifts: int32 [16, 16, 2], replicated, may hold values from -16 to 16, as said below
Outputs:
- best: float32 [256, 512], P('space', 'tm')
- score: float32 [256, 512], P('space', 'tm')
Inputs may be any that keep to these rules, and one draw needn't show every extreme that they name: shifts[v, e, k] = floor(u[v, k] * e / 15) for integer velocities u[v, k] between -16 and 16; u[0] is +16 and u[1] is -16 in both components, so epoch e shifts by at most ceil(16 * e / 15).
All inputs are finite; a program needn't handle non-finite values.
Results may differ from a plain program's by a relative error of at most 0.0048.
Values may be sent and summed in bfloat16 or wider, within the bound.
No kernel may reach another device: no remote copies, remote signals or barrier semaphores. Data moves between devices by JAX's collectives and lax.ppermute only.
A program may use at most 64 MiB of HBM per device.

v0:
```python
import jax
import jax.numpy as jnp
from jax import lax
from jax.sharding import PartitionSpec as P

VELS = 16
RADIUS = 7
MAXSHIFT = 16


def extended(array, sides, width):
    for axis, dim in sides:
        size, length = (lax.axis_size(axis), array.shape[dim])
        up = [(i, (i + 1) % size) for i in range(size - 1)]
        down = [(j, i) for i, j in up]
        last = lax.slice_in_dim(array, length - width, length, axis=dim)
        leading = lax.slice_in_dim(array, 0, width, axis=dim)
        before = lax.ppermute(last, axis, up)
        after = lax.ppermute(leading, axis, down)
        array = jnp.concatenate([before, array, after], axis=dim)
    return array


def filter_frames(padded, kernels):
    return lax.conv_general_dilated(
        padded,
        kernels[:, None],
        (1, 1),
        "VALID",
        dimension_numbers=("CNHW", "OIHW", "CNHW"),
        feature_group_count=2,
        preferred_element_type=jnp.float32,
    )


def on_device(image, inv_var, psf, shifts):
    normed = psf / jnp.sum(psf)
    kernels = jnp.stack([normed.astype(jnp.bfloat16), (normed * normed).astype(jnp.bfloat16)])
    raw = jnp.stack([(image * inv_var).astype(jnp.bfloat16), inv_var.astype(jnp.bfloat16)])
    strips = lax.all_to_all(raw, "space", split_axis=2, concat_axis=1, tiled=True)
    widened = extended(strips, (("tm", 3), ("space", 2)), RADIUS + MAXSHIFT)
    filtered = filter_frames(widened, kernels)
    strip_cols = strips.shape[2]
    strip_rows = strips.shape[3]
    col_pos = (
        lax.axis_index("space") * strip_cols
        - MAXSHIFT
        + jnp.arange(strip_cols + 2 * MAXSHIFT, dtype=jnp.int32)
    )
    row_pos = (
        lax.axis_index("tm") * strip_rows
        - MAXSHIFT
        + jnp.arange(strip_rows + 2 * MAXSHIFT, dtype=jnp.int32)
    )
    col_ok = (col_pos >= 0) & (col_pos < strip_cols * lax.axis_size("space"))
    row_ok = (row_pos >= 0) & (row_pos < strip_rows * lax.axis_size("tm"))
    inside = col_ok[:, None] & row_ok[None, :]
    padded = jnp.where(inside, filtered, 0.0).astype(jnp.bfloat16)
    frames = jnp.moveaxis(padded, 1, 0)
    epoch_shifts = jnp.moveaxis(shifts, 1, 0)
    zero = jnp.zeros((), jnp.int32)

    def cut(frame, shift):
        return lax.dynamic_slice(
            frame, (zero, MAXSHIFT + shift[0], MAXSHIFT + shift[1]), (2, strip_cols, strip_rows)
        )

    per_velocity = jax.vmap(cut, in_axes=(None, 0))

    def visit(carry, inputs):
        upper, lower = carry
        frame, shift_e = inputs
        pieces = per_velocity(frame, shift_e)
        psi_part = pieces[:, 0].astype(jnp.float32)
        phi_part = pieces[:, 1].astype(jnp.float32)
        signal = jnp.abs(psi_part) / jnp.sqrt(jnp.maximum(phi_part, 0.001))
        weight = jax.nn.sigmoid(2.0 * (2.0 - signal))
        return ((upper + weight * psi_part, lower + weight * phi_part), None)

    vels = shifts.shape[0]
    start = (
        jnp.zeros((vels, strip_cols, strip_rows), jnp.float32),
        jnp.zeros((vels, strip_cols, strip_rows), jnp.float32),
    )
    (upper, lower), unused = lax.scan(visit, start, (frames, epoch_shifts))
    like = upper / jnp.sqrt(jnp.maximum(lower, 0.02))
    top = jnp.max(like, axis=0)
    total = jnp.sum(jnp.exp(like), axis=0)
    return (top, jnp.log(total / VELS))


def solution(mesh):
    in_specs = (P("space", None, "tm"), P("space", None, "tm"), P(), P())
    out_specs = (P("space", "tm"), P("space", "tm"))
    return jax.shard_map(
        on_device, mesh=mesh, in_specs=in_specs, out_specs=out_specs, check_vma=False
    )
```

profile of v0, /device:TPU:5, one launch (start us, length us, event | category | flops | bytes accessed | tf_op | source)
XLA Modules:
  0.0 1681.2 jit_solution(16745400224204469672)
XLA Ops:
  2.8 5.5 all-to-all-start
  11.1 6.0 all-to-all-done
  17.3 3.1 collective-permute-start
  20.4 3.1 collective-permute-start.1
  23.5 3.3 collective-permute-done
  26.9 3.7 collective-permute-done.1
  31.9 3.6 collective-permute-start.2
  36.4 2.3 collective-permute-start.3
  39.7 2.9 copy.70
  42.7 4.9 copy.69
  47.6 4.9 copy.71
  52.4 50.3 %fusion.29 = bf16[2,16,78,174]{1,0,3,2:T(2,128)(2,1)S(1)} fusion(bf16[2,16,23,174]{1,0,3,2:T(2,128)(2,1)} %copy.71, bf16[2,16,32,174]{1,0,3,2:T(2,128)(2,1)S(1)} %copy.70, bf16[2,16,23,174]{1,0,3,2:T(2,128)(2,1)} %copy.69), kind=kLoop, calls=%fused_computation.23.clone.clone.clone.1 | loop fusion | flops 868608 | bytes 1737216 | tf_op jit(solution)/shard_map/conv_general_dilated | solution.py:25
  102.7 1030.6 %select_convert_fusion = bf16[16,2,64,160]{0,1,3,2:T(2,128)(2,1)} fusion(pred[64,160]{1,0:T(8,128)(4,1)S(1)} %broadcast_and_fusion, bf16[2,1,15,15]{0,1,3,2:T(2,128)(2,1)S(1)} %copy.73, bf16[2,16,78,174]{1,0,3,2:T(2,128)(2,1)S(1)} %fusion.29), kind=kOutput, calls=%fused_computation.21 | convolution fusion | flops 148111360 | bytes 1535108 | tf_op jit(solution)/shard_map/conv_general_dilated | solution.py:25
  1133.3 11.6 copy.75
  1144.9 535.0 %while.19 = (s32[]{:T(128)}, f32[16,32,128]{2,1,0:T(8,128)S(1)}, f32[16,32,128]{2,1,0:T(8,128)S(1)}, bf16[16,2,64,160]{3,2,1,0:T(8,128)(2,1)S(1)}, s32[16,16,2]{...) while((s32[]{:T(128)}, f32[16,32,128]{2,1,0:T(8,128)S(1)}, f32[16,32,128]{2,1,0:T(8,128)S(1)}, ...), condition=%wide.region_2.3_spmd.clone, body=%wide.region_1.2_spmd.clone.sunk | while | flops 1048805 | bytes 1426640 | solution.py:85
  1145.7 32.4 %while.20 = (s32[]{:T(128)}, bf16[2,64,160]{2,1,0:T(8,128)(2,1)S(1)}, s32[16,3]{0,1:T(4,128)S(1)}, bf16[16,2,32,128]{3,2,0,1:T(8,128)(2,1)S(1)}, s32[]{:T(128)}) while((s32[]{:T(128)}, bf16[2,64,160]{2,1,0:T(8,128)(2,1)S(1)}, s32[16,3]{0,1:T(4,128)S(1)}, bf16[16,2,32,128]{3,2,0,1:T(8,128)(2,1)S(1)}, s32[]{:T(128)}) %tuple.70), condition=%wide.while_cond, body=%wide.while_body.sunk | while | flops 2 | bytes 32885 | solution.py:64
  1146.3 1.4 bitcast_dynamic-update-slice_fusion.2
  1150.4 1.4 bitcast_dynamic-update-slice_fusion.2
  1152.4 1.4 bitcast_dynamic-update-slice_fusion.2
  1154.4 1.4 bitcast_dynamic-update-slice_fusion.2
  1158.5 1.4 bitcast_dynamic-update-slice_fusion.2
  1160.5 1.4 bitcast_dynamic-update-slice_fusion.2
  1162.5 1.4 bitcast_dynamic-update-slice_fusion.2
  1166.6 1.4 bitcast_dynamic-update-slice_fusion.2
  1168.6 1.4 bitcast_dynamic-update-slice_fusion.2
  1170.7 1.4 bitcast_dynamic-update-slice_fusion.2
  1174.7 1.4 bitcast_dynamic-update-slice_fusion.2
  1176.7 1.4 bitcast_dynamic-update-slice_fusion.2
  1179.1 32.4 %while.20 = (s32[]{:T(128)}, bf16[2,64,160]{2,1,0:T(8,128)(2,1)S(1)}, s32[16,3]{0,1:T(4,128)S(1)}, bf16[16,2,32,128]{3,2,0,1:T(8,128)(2,1)S(1)}, s32[]{:T(128)}) while((s32[]{:T(128)}, bf16[2,64,160]{2,1,0:T(8,128)(2,1)S(1)}, s32[16,3]{0,1:T(4,128)S(1)}, bf16[16,2,32,128]{3,2,0,1:T(8,128)(2,1)S(1)}, s32[]{:T(128)}) %tuple.70), condition=%wide.while_cond, body=%wide.while_body.sunk | while | flops 2 | bytes 32885 | solution.py:64
  1179.8 1.4 bitcast_dynamic-update-slice_fusion.2
  1181.8 1.4 bitcast_dynamic-update-slice_fusion.2
  1185.8 1.4 bitcast_dynamic-update-slice_fusion.2
  1187.9 1.4 bitcast_dynamic-update-slice_fusion.2
  1191.9 1.4 bitcast_dynamic-update-slice_fusion.2
  1194.0 1.4 bitcast_dynamic-update-slice_fusion.2
  1196.0 1.4 bitcast_dynamic-update-slice_fusion.2
  1200.0 1.4 bitcast_dynamic-update-slice_fusion.2
  1202.1 1.4 bitcast_dynamic-update-slice_fusion.2
  1204.1 1.4 bitcast_dynamic-update-slice_fusion.2
  1208.2 1.4 bitcast_dynamic-update-slice_fusion.2
  1210.2 1.4 bitcast_dynamic-update-slice_fusion.2
  1212.5 32.4 %while.20 = (s32[]{:T(128)}, bf16[2,64,160]{2,1,0:T(8,128)(2,1)S(1)}, s32[16,3]{0,1:T(4,128)S(1)}, bf16[16,2,32,128]{3,2,0,1:T(8,128)(2,1)S(1)}, s32[]{:T(128)}) while((s32[]{:T(128)}, bf16[2,64,160]{2,1,0:T(8,128)(2,1)S(1)}, s32[16,3]{0,1:T(4,128)S(1)}, bf16[16,2,32,128]{3,2,0,1:T(8,128)(2,1)S(1)}, s32[]{:T(128)}) %tuple.70), condition=%wide.while_cond, body=%wide.while_body.sunk | while | flops 2 | bytes 32885 | solution.py:64
  1213.2 1.4 bitcast_dynamic-update-slice_fusion.2
  1215.2 1.4 bitcast_dynamic-update-slice_fusion.2
  1219.3 1.4 bitcast_dynamic-update-slice_fusion.2
  1221.3 1.4 bitcast_dynamic-update-slice_fusion.2
  1223.3 1.4 bitcast_dynamic-update-slice_fusion.2
  1227.4 1.4 bitcast_dynamic-update-slice_fusion.2
  1229.4 1.4 bitcast_dynamic-update-slice_fusion.2
  1231.5 1.4 bitcast_dynamic-update-slice_fusion.2
  1235.5 1.4 bitcast_dynamic-update-slice_fusion.2
  1246.0 32.4 %while.20 = (s32[]{:T(128)}, bf16[2,64,160]{2,1,0:T(8,128)(2,1)S(1)}, s32[16,3]{0,1:T(4,128)S(1)}, bf16[16,2,32,128]{3,2,0,1:T(8,128)(2,1)S(1)}, s32[]{:T(128)}) while((s32[]{:T(128)}, bf16[2,64,160]{2,1,0:T(8,128)(2,1)S(1)}, s32[16,3]{0,1:T(4,128)S(1)}, bf16[16,2,32,128]{3,2,0,1:T(8,128)(2,1)S(1)}, s32[]{:T(128)}) %tuple.70), condition=%wide.while_cond, body=%wide.while_body.sunk | while | flops 2 | bytes 32885 | solution.py:64
  1279.4 32.4 %while.20 = (s32[]{:T(128)}, bf16[2,64,160]{2,1,0:T(8,128)(2,1)S(1)}, s32[16,3]{0,1:T(4,128)S(1)}, bf16[16,2,32,128]{3,2,0,1:T(8,128)(2,1)S(1)}, s32[]{:T(128)}) while((s32[]{:T(128)}, bf16[2,64,160]{2,1,0:T(8,128)(2,1)S(1)}, s32[16,3]{0,1:T(4,128)S(1)}, bf16[16,2,32,128]{3,2,0,1:T(8,128)(2,1)S(1)}, s32[]{:T(128)}) %tuple.70), condition=%wide.while_cond, body=%wide.while_body.sunk | while | flops 2 | bytes 32885 | solution.py:64
  1312.8 32.4 %while.20 = (s32[]{:T(128)}, bf16[2,64,160]{2,1,0:T(8,128)(2,1)S(1)}, s32[16,3]{0,1:T(4,128)S(1)}, bf16[16,2,32,128]{3,2,0,1:T(8,128)(2,1)S(1)}, s32[]{:T(128)}) while((s32[]{:T(128)}, bf16[2,64,160]{2,1,0:T(8,128)(2,1)S(1)}, s32[16,3]{0,1:T(4,128)S(1)}, bf16[16,2,32,128]{3,2,0,1:T(8,128)(2,1)S(1)}, s32[]{:T(128)}) %tuple.70), condition=%wide.while_cond, body=%wide.while_body.sunk | while | flops 2 | bytes 32885 | solution.py:64
  1346.3 32.4 %while.20 = (s32[]{:T(128)}, bf16[2,64,160]{2,1,0:T(8,128)(2,1)S(1)}, s32[16,3]{0,1:T(4,128)S(1)}, bf16[16,2,32,128]{3,2,0,1:T(8,128)(2,1)S(1)}, s32[]{:T(128)}) while((s32[]{:T(128)}, bf16[2,64,160]{2,1,0:T(8,128)(2,1)S(1)}, s32[16,3]{0,1:T(4,128)S(1)}, bf16[16,2,32,128]{3,2,0,1:T(8,128)(2,1)S(1)}, s32[]{:T(128)}) %tuple.70), condition=%wide.while_cond, body=%wide.while_body.sunk | while | flops 2 | bytes 32885 | solution.py:64
  1379.7 32.4 %while.20 = (s32[]{:T(128)}, bf16[2,64,160]{2,1,0:T(8,128)(2,1)S(1)}, s32[16,3]{0,1:T(4,128)S(1)}, bf16[16,2,32,128]{3,2,0,1:T(8,128)(2,1)S(1)}, s32[]{:T(128)}) while((s32[]{:T(128)}, bf16[2,64,160]{2,1,0:T(8,128)(2,1)S(1)}, s32[16,3]{0,1:T(4,128)S(1)}, bf16[16,2,32,128]{3,2,0,1:T(8,128)(2,1)S(1)}, s32[]{:T(128)}) %tuple.70), condition=%wide.while_cond, body=%wide.while_body.sunk | while | flops 2 | bytes 32885 | solution.py:64
  1413.2 32.4 %while.20 = (s32[]{:T(128)}, bf16[2,64,160]{2,1,0:T(8,128)(2,1)S(1)}, s32[16,3]{0,1:T(4,128)S(1)}, bf16[16,2,32,128]{3,2,0,1:T(8,128)(2,1)S(1)}, s32[]{:T(128)}) while((s32[]{:T(128)}, bf16[2,64,160]{2,1,0:T(8,128)(2,1)S(1)}, s32[16,3]{0,1:T(4,128)S(1)}, bf16[16,2,32,128]{3,2,0,1:T(8,128)(2,1)S(1)}, s32[]{:T(128)}) %tuple.70), condition=%wide.while_cond, body=%wide.while_body.sunk | while | flops 2 | bytes 32885 | solution.py:64
  1446.6 32.4 %while.20 = (s32[]{:T(128)}, bf16[2,64,160]{2,1,0:T(8,128)(2,1)S(1)}, s32[16,3]{0,1:T(4,128)S(1)}, bf16[16,2,32,128]{3,2,0,1:T(8,128)(2,1)S(1)}, s32[]{:T(128)}) while((s32[]{:T(128)}, bf16[2,64,160]{2,1,0:T(8,128)(2,1)S(1)}, s32[16,3]{0,1:T(4,128)S(1)}, bf16[16,2,32,128]{3,2,0,1:T(8,128)(2,1)S(1)}, s32[]{:T(128)}) %tuple.70), condition=%wide.while_cond, body=%wide.while_body.sunk | while | flops 2 | bytes 32885 | solution.py:64
  1480.0 32.4 %while.20 = (s32[]{:T(128)}, bf16[2,64,160]{2,1,0:T(8,128)(2,1)S(1)}, s32[16,3]{0,1:T(4,128)S(1)}, bf16[16,2,32,128]{3,2,0,1:T(8,128)(2,1)S(1)}, s32[]{:T(128)}) while((s32[]{:T(128)}, bf16[2,64,160]{2,1,0:T(8,128)(2,1)S(1)}, s32[16,3]{0,1:T(4,128)S(1)}, bf16[16,2,32,128]{3,2,0,1:T(8,128)(2,1)S(1)}, s32[]{:T(128)}) %tuple.70), condition=%wide.while_cond, body=%wide.while_body.sunk | while | flops 2 | bytes 32885 | solution.py:64
  1513.5 32.4 %while.20 = (s32[]{:T(128)}, bf16[2,64,160]{2,1,0:T(8,128)(2,1)S(1)}, s32[16,3]{0,1:T(4,128)S(1)}, bf16[16,2,32,128]{3,2,0,1:T(8,128)(2,1)S(1)}, s32[]{:T(128)}) while((s32[]{:T(128)}, bf16[2,64,160]{2,1,0:T(8,128)(2,1)S(1)}, s32[16,3]{0,1:T(4,128)S(1)}, bf16[16,2,32,128]{3,2,0,1:T(8,128)(2,1)S(1)}, s32[]{:T(128)}) %tuple.70), condition=%wide.while_cond, body=%wide.while_body.sunk | while | flops 2 | bytes 32885 | solution.py:64
  1546.9 32.4 %while.20 = (s32[]{:T(128)}, bf16[2,64,160]{2,1,0:T(8,128)(2,1)S(1)}, s32[16,3]{0,1:T(4,128)S(1)}, bf16[16,2,32,128]{3,2,0,1:T(8,128)(2,1)S(1)}, s32[]{:T(128)}) while((s32[]{:T(128)}, bf16[2,64,160]{2,1,0:T(8,128)(2,1)S(1)}, s32[16,3]{0,1:T(4,128)S(1)}, bf16[16,2,32,128]{3,2,0,1:T(8,128)(2,1)S(1)}, s32[]{:T(128)}) %tuple.70), condition=%wide.while_cond, body=%wide.while_body.sunk | while | flops 2 | bytes 32885 | solution.py:64
  1580.3 32.4 %while.20 = (s32[]{:T(128)}, bf16[2,64,160]{2,1,0:T(8,128)(2,1)S(1)}, s32[16,3]{0,1:T(4,128)S(1)}, bf16[16,2,32,128]{3,2,0,1:T(8,128)(2,1)S(1)}, s32[]{:T(128)}) while((s32[]{:T(128)}, bf16[2,64,160]{2,1,0:T(8,128)(2,1)S(1)}, s32[16,3]{0,1:T(4,128)S(1)}, bf16[16,2,32,128]{3,2,0,1:T(8,128)(2,1)S(1)}, s32[]{:T(128)}) %tuple.70), condition=%wide.while_cond, body=%wide.while_body.sunk | while | flops 2 | bytes 32885 | solution.py:64
  1613.8 32.4 %while.20 = (s32[]{:T(128)}, bf16[2,64,160]{2,1,0:T(8,128)(2,1)S(1)}, s32[16,3]{0,1:T(4,128)S(1)}, bf16[16,2,32,128]{3,2,0,1:T(8,128)(2,1)S(1)}, s32[]{:T(128)}) while((s32[]{:T(128)}, bf16[2,64,160]{2,1,0:T(8,128)(2,1)S(1)}, s32[16,3]{0,1:T(4,128)S(1)}, bf16[16,2,32,128]{3,2,0,1:T(8,128)(2,1)S(1)}, s32[]{:T(128)}) %tuple.70), condition=%wide.while_cond, body=%wide.while_body.sunk | while | flops 2 | bytes 32885 | solution.py:64
  1647.2 32.4 %while.20 = (s32[]{:T(128)}, bf16[2,64,160]{2,1,0:T(8,128)(2,1)S(1)}, s32[16,3]{0,1:T(4,128)S(1)}, bf16[16,2,32,128]{3,2,0,1:T(8,128)(2,1)S(1)}, s32[]{:T(128)}) while((s32[]{:T(128)}, bf16[2,64,160]{2,1,0:T(8,128)(2,1)S(1)}, s32[16,3]{0,1:T(4,128)S(1)}, bf16[16,2,32,128]{3,2,0,1:T(8,128)(2,1)S(1)}, s32[]{:T(128)}) %tuple.70), condition=%wide.while_cond, body=%wide.while_body.sunk | while | flops 2 | bytes 32885 | solution.py:64
  (877 shorter events, 495.8 us)
Async XLA Ops:
  0.6 38.3 %copy-start.2 = (s32[16,16,2]{1,2,0:T(2,128)S(1)}, s32[16,16,2]{1,2,0:T(2,128)}, u32[]{:S(2)}) copy-start(s32[16,16,2]{1,2,0:T(2,128)} %param.9) | copy-start | bytes 6148
  2.8 14.3 all-to-all-start
  17.3 9.6 collective-permute-start
  20.4 10.2 collective-permute-start.1
  31.9 10.7 collective-permute-start.2
  36.4 11.2 collective-permute-start.3
  102.7 1042.2 %copy-start = (f32[16,32,128]{2,1,0:T(8,128)S(1)}, f32[16,32,128]{2,1,0:T(8,128)}, u32[]{:S(2)}) copy-start(f32[16,32,128]{2,1,0:T(8,128)} %custom-call) | copy-start | bytes 786436
  102.7 1042.2 %copy-start.1 = (f32[16,32,128]{2,1,0:T(8,128)S(1)}, f32[16,32,128]{2,1,0:T(8,128)}, u32[]{:S(2)}) copy-start(f32[16,32,128]{2,1,0:T(8,128)} %custom-call.1) | copy-start | bytes 786436
where the time goes:
time: 1690 us; the launch traced here: 1680 us
  matrix products  1030 us (61%)
  local copies, waits for them, and re-layouts  555 us (33%)
  other arithmetic  59.7 us (4%)
  starting transfers between devices  17.6 us (1%)
    conv_general_dilated x1, matrix products, filter_frames(): lax.conv_general_dilated(padded, kernels[:, None], (1, 1), 'VALID', dimen...  1030 us
    gather x768, local copies, waits for them, and re-layouts  516 us
    conv_general_dilated x1, other arithmetic, filter_frames(): lax.conv_general_dilated(padded, kernels[:, None], (1, 1), 'VALID', dimen...  50.3 us
  transfers between devices with their start and end apart: 5, of which 3 were waited for; matrix products, arithmetic and copies ran while one was open for 1% of the time, Pallas kernels for 0%

commit v1 on v0

v1 whole, which is shorter than its diff:
```python
import functools

import jax
import jax.numpy as jnp
from jax import lax
from jax.experimental import pallas as pl
from jax.experimental.pallas import tpu as pltpu
from jax.sharding import PartitionSpec as P

RADIUS = 7
TAPS = 2 * RADIUS + 1
MAXSHIFT = 16
LANES = 128
HALO = 24
BLOCK = 256
F32 = jnp.float32
BF16 = jnp.bfloat16
VMEM = pl.BlockSpec(memory_space=pltpu.VMEM)
SMEM = pl.BlockSpec(memory_space=pltpu.SMEM)
PARAMS = pltpu.CompilerParams(vmem_limit_bytes=48 * 1024 * 1024)


def prepare_kernel(image_ref, inv_var_ref, main_ref, first_ref, last_ref):
    epochs, _, rows = image_ref.shape
    for ep in range(epochs):
        inv_var = inv_var_ref[ep]
        for plane, values in ((0, image_ref[ep] * inv_var), (1, inv_var)):
            turned = values.T.astype(BF16)
            main_ref[plane, ep] = turned
            first_ref[plane, ep] = turned[:HALO]
            last_ref[plane, ep] = turned[rows - HALO :]


def prepare(image, inv_var):
    epochs, width, rows = image.shape
    halo = jax.ShapeDtypeStruct((2, epochs, HALO, width), BF16)
    return pl.pallas_call(
        prepare_kernel,
        out_shape=(jax.ShapeDtypeStruct((2, epochs, rows, width), BF16), halo, halo),
        in_specs=[VMEM] * 2,
        out_specs=[VMEM] * 3,
        compiler_params=PARAMS,
        name="prepare",
    )(image, inv_var)


def band_kernel(psf_ref, band_ref, corner_ref):
    psf = psf_ref[...]
    normed = psf / jnp.sum(psf)
    flip = (
        lax.broadcasted_iota(jnp.int32, (TAPS, LANES), 0)
        + lax.broadcasted_iota(jnp.int32, (TAPS, LANES), 1)
        == TAPS - 1
    ).astype(BF16)
    size = (LANES, LANES)
    ahead = lax.broadcasted_iota(jnp.int32, size, 1) - lax.broadcasted_iota(jnp.int32, size, 0)
    near = jnp.abs(ahead) <= LANES // 2
    below = ahead > LANES // 2
    above = ahead < -(LANES // 2)
    for plane, kern in ((0, normed.astype(BF16)), (1, (normed * normed).astype(BF16))):
        taps = lax.dot_general(kern, flip, (((0,), (0,)), ((), ())), preferred_element_type=F32)
        for j in range(TAPS):
            spread = jnp.broadcast_to(taps[j : j + 1, :], size)
            ring = pltpu.roll(spread, LANES - RADIUS, 1, stride=1, stride_axis=0)
            diagonal = jnp.where(near, ring, 0.0).astype(BF16)
            at = j * BLOCK
            band_ref[plane, at : at + LANES, :LANES] = diagonal
            band_ref[plane, at + LANES : at + BLOCK, LANES:] = diagonal
            from_left = jnp.where(above, ring, 0.0).astype(BF16)
            from_right = jnp.where(below, ring, 0.0).astype(BF16)
            band_ref[plane, at : at + LANES, LANES:] = from_left
            band_ref[plane, at + LANES : at + BLOCK, :LANES] = from_right
            corner_ref[plane, 0, j * LANES : (j + 1) * LANES] = from_left
            corner_ref[plane, 1, j * LANES : (j + 1) * LANES] = from_right


def band_matrices(psf):
    return pl.pallas_call(
        band_kernel,
        out_shape=(
            jax.ShapeDtypeStruct((2, TAPS * BLOCK, BLOCK), BF16),
            jax.ShapeDtypeStruct((2, 2, TAPS * LANES, LANES), BF16),
        ),
        in_specs=[VMEM],
        out_specs=[VMEM] * 2,
        compiler_params=PARAMS,
        name="band",
    )(psf)


def filter_kernel(chips, where_ref, main_ref, before_ref, after_ref, band_ref, corner_ref, *refs):
    outs, (tall, lhs, corner_lhs, turned, wide) = refs[:chips], refs[chips:]
    _, epochs, rows, width = main_ref.shape
    out_rows = rows + 2 * MAXSHIFT
    for plane in range(2):
        for ep in range(epochs):
            tall[plane, ep, :HALO] = before_ref[plane, ep]
            tall[plane, ep, HALO : HALO + rows] = main_ref[plane, ep]
            tall[plane, ep, HALO + rows :] = after_ref[plane, ep]
    chip, row_block, height = where_ref[0], where_ref[1], where_ref[2]
    row = row_block * rows - MAXSHIFT + lax.broadcasted_iota(jnp.int32, (out_rows, BLOCK), 0)
    inside = (row >= 0) & (row < height)
    skip = HALO - MAXSHIFT - RADIUS
    blocks = width // BLOCK
    for block in range(blocks):
        at = block * BLOCK
        filtered = []
        for plane in range(2):
            for ep in range(epochs):
                for j in range(TAPS):
                    lhs[ep * out_rows : (ep + 1) * out_rows, j * BLOCK : (j + 1) * BLOCK] = tall[
                        plane, ep, skip + j : skip + j + out_rows, at : at + BLOCK
                    ]
            total = jnp.dot(lhs[...], band_ref[plane], preferred_element_type=F32)
            low, high = total[:, :LANES], total[:, LANES:]
            for side, source in ((0, at - LANES), (1, at + BLOCK)):
                if source < 0 or source >= width:
                    continue
                for ep in range(epochs):
                    for j in range(TAPS):
                        corner_lhs[ep * out_rows : (ep + 1) * out_rows, j * LANES : (j + 1) * LANES] = tall[
                            plane, ep, skip + j : skip + j + out_rows, source : source + LANES
                        ]
                more = jnp.dot(corner_lhs[...], corner_ref[plane, side], preferred_element_type=F32)
                low, high = (low + more, high) if side == 0 else (low, high + more)
            total = jnp.concatenate([low, high], axis=1)
            parts = []
            for ep in range(epochs):
                part = total[ep * out_rows : (ep + 1) * out_rows]
                parts.append(jnp.where(inside, part.astype(BF16).astype(F32), 0.0))
            filtered.append(parts)
        for ep in range(epochs):
            psi, phi = filtered[0][ep], filtered[1][ep]
            signal = jnp.abs(psi) * lax.rsqrt(jnp.maximum(phi, 0.001))
            weight = 1.0 / (1.0 + jnp.exp(2.0 * signal - 4.0))
            for plane, values in ((0, weight * psi), (1, weight * phi)):
                slot = 2 * ep + plane
                turn = (MAXSHIFT * 2 * slot) % rows
                base = slot * LANES
                turned[base + turn : base + rows, :] = values[: rows - turn]
                if turn:
                    turned[base : base + turn, :] = values[rows - turn : rows]
                extra = 2 * epochs * LANES + slot * 2 * MAXSHIFT
                turned[extra : extra + 2 * MAXSHIFT, :] = values[rows:]
        for part in range(2 * epochs + 1):
            lanes = slice(part * LANES, (part + 1) * LANES)
            wide[MAXSHIFT + at : MAXSHIFT + at + BLOCK, lanes] = turned[lanes, :].T.astype(BF16)
    edge = jnp.zeros((MAXSHIFT, wide.shape[1]), BF16)
    wide[:MAXSHIFT] = edge
    wide[MAXSHIFT + width :] = edge
    span = width // chips
    for k in range(chips):
        other = jnp.bitwise_xor(chip, k)
        start = pl.multiple_of(other * span, span)
        outs[k][...] = wide[pl.ds(start, span + 2 * MAXSHIFT), :]


def filter_epochs(where, main, before, after, band, corner, chips):
    _, epochs, rows, width = main.shape
    out_rows = rows + 2 * MAXSHIFT
    lanes = (2 * epochs + 1) * LANES
    piece = jax.ShapeDtypeStruct((width // chips + 2 * MAXSHIFT, lanes), BF16)
    return pl.pallas_call(
        functools.partial(filter_kernel, chips),
        out_shape=(piece,) * chips,
        in_specs=[SMEM] + [VMEM] * 5,
        out_specs=[VMEM] * chips,
        scratch_shapes=[
            pltpu.VMEM((2, epochs, rows + 2 * HALO, width), BF16),
            pltpu.VMEM((epochs * out_rows, TAPS * BLOCK), BF16),
            pltpu.VMEM((epochs * out_rows, TAPS * LANES), BF16),
            pltpu.VMEM((lanes, BLOCK), F32),
            pltpu.VMEM((width + 2 * MAXSHIFT, lanes), BF16),
        ],
        compiler_params=PARAMS,
        name="filter",
    )(where, main, before, after, band, corner)


def stack_kernel(chips, vels, where_ref, shifts_ref, *refs):
    pieces, (best_ref, score_ref), (frames,) = refs[: 2 * chips], refs[2 * chips : -1], refs[-1:]
    chip, core = where_ref[0], where_ref[3]
    cols, rows = best_ref.shape
    window = cols + 2 * MAXSHIFT
    parts = pieces[0].shape[1] // LANES
    epochs = (parts - 1) // 2
    start = pl.multiple_of(core * cols, cols)
    for slot in range(2 * chips):
        for part in range(parts):
            base = (slot * parts + part) * window
            frames[base : base + window] = pieces[slot][
                pl.ds(start, window), part * LANES : (part + 1) * LANES
            ].astype(F32)
    lane = lax.broadcasted_iota(jnp.int32, (cols, LANES), 1)

    def add_slot(slot, v, upper, lower):
        if isinstance(slot, int):
            k, flip = slot // 2, slot % 2
        else:
            k, flip = lax.div(slot, 2), lax.rem(slot, 2)
        owner = 2 * jnp.bitwise_xor(chip, k) + jnp.bitwise_xor(core, flip)
        for ep in range(epochs):
            epoch = owner * epochs + ep
            right = MAXSHIFT + shifts_ref[2 * v, epoch]
            down = MAXSHIFT + shifts_ref[2 * v + 1, epoch]
            base = slot * (parts * window) + right
            extra = frames[pl.ds(base + 2 * epochs * window, cols), :]
            sums = []
            for plane, total in ((0, upper), (1, lower)):
                part = 2 * ep + plane
                turn = 2 * MAXSHIFT * part
                place = lane if turn == 0 else lax.rem(lane + (LANES - turn), LANES)
                held = frames[pl.ds(base + part * window, cols), :]
                merged = jnp.where(place < down, extra, held)
                sums.append(total + pltpu.roll(merged, lax.rem(2 * LANES - turn - down, LANES), 1))
            upper, lower = sums
        return upper, lower

    def visit(v, carry):
        top, total = carry
        upper = jnp.zeros((cols, LANES), F32)
        lower = jnp.zeros((cols, LANES), F32)
        group = 8
        if 2 * chips <= group:
            for slot in range(2 * chips):
                upper, lower = add_slot(slot, v, upper, lower)
        else:
            def some(g, sums):
                for s in range(group):
                    sums = add_slot(g * group + s, v, *sums)
                return sums

            upper, lower = lax.fori_loop(0, 2 * chips // group, some, (upper, lower))
        like = upper * lax.rsqrt(jnp.maximum(lower, 0.02))
        return jnp.maximum(top, like), total + jnp.exp(like)

    top = jnp.full((cols, LANES), -jnp.inf, F32)
    top, total = lax.fori_loop(0, vels, visit, (top, jnp.zeros((cols, LANES), F32)))
    best_ref[...] = top
    score_ref[...] = jnp.log(total / vels)


def stack_epochs(where, shifts, pieces, cols, rows):
    vels = shifts.shape[0] // 2
    chips = len(pieces) // 2
    parts = pieces[0].shape[1] // LANES
    out = jax.ShapeDtypeStruct((cols, rows), F32)
    return pl.pallas_call(
        functools.partial(stack_kernel, chips, vels),
        out_shape=(out, out),
        in_specs=[SMEM] * 2 + [VMEM] * (2 * chips),
        out_specs=[VMEM] * 2,
        scratch_shapes=[pltpu.VMEM((2 * chips * parts * (cols + 2 * MAXSHIFT), LANES), F32)],
        compiler_params=PARAMS,
        name="stack",
    )(where, shifts, *pieces)


def on_device(image, inv_var, psf, shifts):
    epochs, width, rows = image.shape
    devices = lax.axis_size("space")
    row_blocks = lax.axis_size("tm")
    chips = devices // 2
    place, row_block = lax.axis_index("space"), lax.axis_index("tm")
    where = jnp.stack([place // 2, row_block, rows * row_blocks, place % 2]).astype(jnp.int32)
    table = jnp.transpose(shifts, (0, 2, 1)).reshape(2 * shifts.shape[0], shifts.shape[1])

    main, first, last = prepare(image, inv_var)
    up = [(i, i + 1) for i in range(row_blocks - 1)]
    down = [(j, i) for i, j in up]
    before = lax.ppermute(last, "tm", up)
    after = lax.ppermute(first, "tm", down)
    band, corner = band_matrices(psf)
    sent = filter_epochs(where, main, before, after, band, corner, chips)

    swap = [(i, i ^ 1) for i in range(devices)]
    got = {0: sent[0]}
    for k in reversed(range(1, chips)):
        pairs = [(2 * i + c, 2 * (i ^ k) + c) for i in range(chips) for c in range(2)]
        got[k] = lax.ppermute(sent[k], "space", pairs)
    pieces = []
    for k in range(chips):
        pieces += [got[k], lax.ppermute(got[k], "space", swap)]
    return stack_epochs(where, table, pieces, width // devices, rows)


def solution(mesh):
    in_specs = (P("space", None, "tm"), P("space", None, "tm"), P(), P())
    out_specs = (P("space", "tm"), P("space", "tm"))
    return jax.shard_map(
        on_device, mesh=mesh, in_specs=in_specs, out_specs=out_specs, check_vma=False
    )
```

time: 1690 us -> 37.7 us (0.02)
  matrix products: 1030 us -> 0 us
  local copies, waits for them, and re-layouts: 555 us -> 4.45 us
  other arithmetic: 59.7 us -> 0.08 us
    conv_general_dilated x1 -> x0, matrix products: 1030 us -> none  [filter_frames(): lax.conv_general_dilated(padded, kernels[:, None], (1, 1), 'VALID', dimen...]
    gather x768 -> x0, local copies, waits for them, and re-layouts: 516 us -> none
    conv_general_dilated x1 -> x0, other arithmetic: 50.3 us -> none  [filter_frames(): lax.conv_general_dilated(padded, kernels[:, None], (1, 1), 'VALID', dimen...]
  transfers between devices with their start and end apart: 5 -> 9, of which waited for: 3 -> 2; matrix products, arithmetic and copies ran while one was open for 1% -> 0% of each run, Pallas kernels for 0% -> 3%
where the time goes in v1:
time: 37.7 us; the launch traced here: 37.4 us
  starting transfers between devices  20.8 us (55%)
  Pallas kernels  10 us (27%)
  local copies, waits for them, and re-layouts  4.45 us (12%)
  waiting for transfers between devices  1.34 us (4%)
  between operations  0.72 us (2%)
    ppermute x4, starting transfers between devices, on_device(): pieces += [got[k], lax.ppermute(got[k], 'space', swap)]  11 us
    pallas_call x1, Pallas kernels, stack_epochs(): pl.pallas_call(functools.partial(stack_kernel, chips, vels), out_shape=(o...  5.11 us
    unnamed x10, local copies, waits for them, and re-layouts  4.45 us
    pallas_call x1, Pallas kernels, filter_epochs(): pl.pallas_call(functools.partial(filter_kernel, chips), out_shape=(piece,...  3.85 us
    ppermute x3, starting transfers between devices, on_device(): got[k] = lax.ppermute(sent[k], 'space', pairs)  3.67 us
    ppermute x1, starting transfers between devices, on_device(): before = lax.ppermute(last, 'tm', up)  3.12 us
    ppermute x1, starting transfers between devices, on_device(): after = lax.ppermute(first, 'tm', down)  3.06 us
    ppermute x4, waiting for transfers between devices, on_device(): pieces += [got[k], lax.ppermute(got[k], 'space', swap)]  1.32 us
  transfers between devices with their start and end apart: 9, of which 2 were waited for; matrix products, arithmetic and copies ran while one was open for 0% of the time, Pallas kernels for 3%

profile of v1, /device:TPU:5, one launch (start us, length us, event | category | flops | bytes accessed | tf_op | source)
XLA Modules:
  0.0 37.4 jit_solution(15120965406328310730)
XLA Ops:
  0.6 0.0 copy-start.1
  0.6 0.9 %copy-done.1 = f32[2,256,128]{2,1,0:T(8,128)S(1)} copy-done((f32[2,256,128]{2,1,0:T(8,128)S(1)}, f32[2,256,128]{2,1,0:T(8,128)}, u32[]{:S(2)}) %copy-start.1) | copy-done | bytes 262168
  1.6 0.0 copy-start.2
  1.6 0.9 %copy-done.2 = f32[2,256,128]{2,1,0:T(8,128)S(1)} copy-done((f32[2,256,128]{2,1,0:T(8,128)S(1)}, f32[2,256,128]{2,1,0:T(8,128)}, u32[]{:S(2)}) %copy-start.2) | copy-done | bytes 262168
  2.5 0.0 copy-start.3
  2.5 0.1 prepare.1
  2.7 3.1 %collective-permute-start = (bf16[2,2,24,256]{3,2,1,0:T(8,128)(2,1)S(1)}, bf16[2,2,24,256]{3,2,1,0:T(8,128)(2,1)S(1)}, u32[]{:S(2)}, u32[]{:S(2)}) collective-permute-start(bf16[2,2,24,256]{3,2,1,0:T(8,128)(2,1)S(1)} %get-tuple-element.12), channel_id=1, source_target_pairs={{0,8},{8,16},{16,24},{1,9},{9,17},{17,25},{2,10},{10,18},{18,26},{... | collective-permute-start | bytes 147464 | tf_op jit(solution)/shard_map/ppermute | solution.py:271
  5.8 3.1 %collective-permute-start.1 = (bf16[2,2,24,256]{3,2,1,0:T(8,128)(2,1)S(1)}, bf16[2,2,24,256]{3,2,1,0:T(8,128)(2,1)S(1)}, u32[]{:S(2)}, u32[]{:S(2)}) collective-permute-start(bf16[2,2,24,256]{3,2,1,0:T(8,128)(2,1)S(1)} %get-tuple-element.13), channel_id=1, source_target_pairs={{8,0},{16,8},{24,16},{9,1},{17,9},{25,17},{10,2},{18,10},{26,18},{... | collective-permute-start | bytes 147464 | tf_op jit(solution)/shard_map/ppermute | solution.py:272
  8.9 0.1 pad_add_fusion.where_ref
  9.0 0.0 copy-start.4
  9.0 0.7 %copy-done.4 = f32[15,15]{1,0:T(8,128)S(1)} copy-done((f32[15,15]{1,0:T(8,128)S(1)}, f32[15,15]{1,0:T(8,128)}, u32[]{:S(2)}) %copy-start.4) | copy-done | bytes 924
  9.7 0.9 %band.1 = (bf16[2,3840,256]{2,1,0:T(8,128)(2,1)S(1)}, bf16[2,2,1920,128]{3,2,1,0:T(8,128)(2,1)S(1)}) custom-call(f32[15,15]{1,0:T(8,128)S(1)} %copy-done.4), custom_call_target="tpu_custom_call" | custom-call | tf_op jit(solution)/shard_map/band/pallas_call | solution.py:78
  10.6 0.0 copy-start
  10.6 1.9 %copy-done = bf16[2,3840,256]{2,1,0:T(8,128)(2,1)} copy-done((bf16[2,3840,256]{2,1,0:T(8,128)(2,1)}, bf16[2,3840,256]{2,1,0:T(8,128)(2,1)S(1)}, u32[]{:S(2)}) %copy-start) | copy-done | bytes 3932184
  12.5 0.0 collective-permute-done.before_ref
  12.5 0.0 collective-permute-done.1.after_ref
  12.5 3.8 %filter.1 = (bf16[96,640]{1,0:T(8,128)(2,1)S(1)}, bf16[96,640]{1,0:T(8,128)(2,1)S(1)}, bf16[96,640]{1,0:T(8,128)(2,1)S(1)}, bf16[96,640]{1,0:T(8,128)(2,1)S(1)}) custom-call(s32[4]{0:T(128)S(1)} %pad_add_fusion.where_ref, bf16[2,2,128,256]{3,2,1,0:T(8,128)(2,1)S(1)} %get-tuple-element.11.main_ref, ...), custom_call_target="tpu_custom_call" | custom-call | tf_op jit(solution)/shard_map/filter/pallas_call | solution.py:163
  16.3 1.4 %collective-permute-start.3 = (bf16[96,640]{1,0:T(8,128)(2,1)S(1)}, bf16[96,640]{1,0:T(8,128)(2,1)S(1)}, u32[]{:S(2)}, u32[]{:S(2)}) collective-permute-start(bf16[96,640]{1,0:T(8,128)(2,1)S(1)} %get-tuple-element.17), channel_id=1, source_target_pairs={{0,2},{1,3},{2,0},{3,1},{4,6},{5,7},{6,4},{7,5},{8,10},{9,11},{10,... | collective-permute-start | bytes 368648 | tf_op jit(solution)/shard_map/ppermute | solution.py:280
  17.7 2.3 %collective-permute-start.5 = (bf16[96,640]{1,0:T(8,128)(2,1)S(1)}, bf16[96,640]{1,0:T(8,128)(2,1)S(1)}, u32[]{:S(2)}, u32[]{:S(2)}) collective-permute-start(bf16[96,640]{1,0:T(8,128)(2,1)S(1)} %get-tuple-element.18), channel_id=1, source_target_pairs={{0,4},{1,5},{2,6},{3,7},{4,0},{5,1},{6,2},{7,3},{8,12},{9,13},{10,... | collective-permute-start | bytes 368648 | tf_op jit(solution)/shard_map/ppermute | solution.py:280
  20.0 0.0 collective-permute-start.7
  20.0 2.0 %collective-permute-start.2 = (bf16[96,640]{1,0:T(8,128)(2,1)S(1)}, bf16[96,640]{1,0:T(8,128)(2,1)S(1)}, u32[]{:S(2)}, u32[]{:S(2)}) collective-permute-start(bf16[96,640]{1,0:T(8,128)(2,1)S(1)} %get-tuple-element.16.refs_0_), channel_id=1, source_target_pairs={{0,1},{1,0},{2,3},{3,2},{4,5},{5,4},{6,7},{7,6},{8,9},{9,8},{10,11... | collective-permute-start | bytes 368648 | tf_op jit(solution)/shard_map/ppermute | solution.py:283
  22.0 0.0 collective-permute-done.3.refs_2_
  22.0 1.8 %collective-permute-start.4 = (bf16[96,640]{1,0:T(8,128)(2,1)S(1)}, bf16[96,640]{1,0:T(8,128)(2,1)S(1)}, u32[]{:S(2)}, u32[]{:S(2)}) collective-permute-start(bf16[96,640]{1,0:T(8,128)(2,1)S(1)} %collective-permute-done.3.refs_2_), channel_id=1, source_target_pairs={{0,1},{1,0},{2,3},{3,2},{4,5},{5,4},{6,7},{7,6},{8,9},{9,8},{10,11... | collective-permute-start | bytes 368648 | tf_op jit(solution)/shard_map/ppermute | solution.py:283
  23.8 0.0 collective-permute-done.5.refs_4_
  23.8 7.1 %collective-permute-start.6 = (bf16[96,640]{1,0:T(8,128)(2,1)S(1)}, bf16[96,640]{1,0:T(8,128)(2,1)S(1)}, u32[]{:S(2)}, u32[]{:S(2)}) collective-permute-start(bf16[96,640]{1,0:T(8,128)(2,1)S(1)} %collective-permute-done.5.refs_4_), channel_id=1, source_target_pairs={{0,1},{1,0},{2,3},{3,2},{4,5},{5,4},{6,7},{7,6},{8,9},{9,8},{10,11... | collective-permute-start | bytes 368648 | tf_op jit(solution)/shard_map/ppermute | solution.py:283
  31.0 0.0 collective-permute-done.7.refs_6_
  31.0 0.0 collective-permute-start.8
  31.0 0.0 collective-permute-done.2.refs_1_
  31.0 0.0 collective-permute-done.4.refs_3_
  31.0 1.0 %collective-permute-done.6.refs_5_ = bf16[96,640]{1,0:T(8,128)(2,1)S(1)} collective-permute-done((bf16[96,640]{1,0:T(8,128)(2,1)S(1)}, bf16[96,640]{1,0:T(8,128)(2,1)S(1)}, u32[]{:S(2)}, u32[]{:S(2)}) %collective-permute-start.6) | collective-permute-done | bytes 122912 | tf_op jit(solution)/shard_map/ppermute | solution.py:283
  31.9 0.4 collective-permute-done.8.refs_7_
  32.3 0.0 copy-done.3
  32.3 5.1 %stack.17 = (f32[32,128]{1,0:T(8,128)}, f32[32,128]{1,0:T(8,128)}) custom-call(s32[4]{0:T(128)S(1)} %pad_add_fusion.where_ref, s32[32,16]{1,0:T(8,128)S(1)} %bitcast.6, bf16[96,640]{1,0:T(8,128)(2,1)S(1)} %get-tuple-element.16.refs_0_, bf16[96,640]{1,0:T(8,128)(2,1)S(1)} %collective-permute-done.2.refs_1_, ...), custom_call_target="tpu_custom_call" | custom-call | tf_op jit(solution)/shard_map/stack/pallas_call | solution.py:248
Async XLA Ops:
  0.6 1.0 %copy-start.1 = (f32[2,256,128]{2,1,0:T(8,128)S(1)}, f32[2,256,128]{2,1,0:T(8,128)}, u32[]{:S(2)}) copy-start(f32[2,256,128]{2,1,0:T(8,128)} %image_ref.1) | copy-start | bytes 786436
  1.6 0.9 %copy-start.2 = (f32[2,256,128]{2,1,0:T(8,128)S(1)}, f32[2,256,128]{2,1,0:T(8,128)}, u32[]{:S(2)}) copy-start(f32[2,256,128]{2,1,0:T(8,128)} %inv_var_ref.1) | copy-start | bytes 786436
  2.5 29.8 %copy-start.3 = (s32[16,16,2]{1,2,0:T(2,128)S(1)}, s32[16,16,2]{1,2,0:T(2,128)}, u32[]{:S(2)}) copy-start(s32[16,16,2]{1,2,0:T(2,128)} %param.7) | copy-start | bytes 6148
  2.7 9.8 %collective-permute-start = (bf16[2,2,24,256]{3,2,1,0:T(8,128)(2,1)S(1)}, bf16[2,2,24,256]{3,2,1,0:T(8,128)(2,1)S(1)}, u32[]{:S(2)}, u32[]{:S(2)}) collective-permute-start(bf16[2,2,24,256]{3,2,1,0:T(8,128)(2,1)S(1)} %get-tuple-element.12), channel_id=1, source_target_pairs={{0,8},{8,16},{16,24},{1,9},{9,17},{17,25},{2,10},{10,18},{18,26},{... | collective-permute-start | bytes 147464 | tf_op jit(solution)/shard_map/ppermute | solution.py:271
  5.8 6.7 %collective-permute-start.1 = (bf16[2,2,24,256]{3,2,1,0:T(8,128)(2,1)S(1)}, bf16[2,2,24,256]{3,2,1,0:T(8,128)(2,1)S(1)}, u32[]{:S(2)}, u32[]{:S(2)}) collective-permute-start(bf16[2,2,24,256]{3,2,1,0:T(8,128)(2,1)S(1)} %get-tuple-element.13), channel_id=1, source_target_pairs={{8,0},{16,8},{24,16},{9,1},{17,9},{25,17},{10,2},{18,10},{26,18},{... | collective-permute-start | bytes 147464 | tf_op jit(solution)/shard_map/ppermute | solution.py:272
  9.0 0.7 %copy-start.4 = (f32[15,15]{1,0:T(8,128)S(1)}, f32[15,15]{1,0:T(8,128)}, u32[]{:S(2)}) copy-start(f32[15,15]{1,0:T(8,128)} %psf_ref.1) | copy-start | bytes 2704
  10.6 1.9 %copy-start = (bf16[2,3840,256]{2,1,0:T(8,128)(2,1)}, bf16[2,3840,256]{2,1,0:T(8,128)(2,1)S(1)}, u32[]{:S(2)}) copy-start(bf16[2,3840,256]{2,1,0:T(8,128)(2,1)S(1)} %get-tuple-element.14.band_ref) | copy-start | bytes 11796484
  16.3 5.7 %collective-permute-start.3 = (bf16[96,640]{1,0:T(8,128)(2,1)S(1)}, bf16[96,640]{1,0:T(8,128)(2,1)S(1)}, u32[]{:S(2)}, u32[]{:S(2)}) collective-permute-start(bf16[96,640]{1,0:T(8,128)(2,1)S(1)} %get-tuple-element.17), channel_id=1, source_target_pairs={{0,2},{1,3},{2,0},{3,1},{4,6},{5,7},{6,4},{7,5},{8,10},{9,11},{10,... | collective-permute-start | bytes 368648 | tf_op jit(solution)/shard_map/ppermute | solution.py:280
  17.7 6.1 %collective-permute-start.5 = (bf16[96,640]{1,0:T(8,128)(2,1)S(1)}, bf16[96,640]{1,0:T(8,128)(2,1)S(1)}, u32[]{:S(2)}, u32[]{:S(2)}) collective-permute-start(bf16[96,640]{1,0:T(8,128)(2,1)S(1)} %get-tuple-element.18), channel_id=1, source_target_pairs={{0,4},{1,5},{2,6},{3,7},{4,0},{5,1},{6,2},{7,3},{8,12},{9,13},{10,... | collective-permute-start | bytes 368648 | tf_op jit(solution)/shard_map/ppermute | solution.py:280
  20.0 11.0 %collective-permute-start.7 = (bf16[96,640]{1,0:T(8,128)(2,1)S(1)}, bf16[96,640]{1,0:T(8,128)(2,1)S(1)}, u32[]{:S(2)}, u32[]{:S(2)}) collective-permute-start(bf16[96,640]{1,0:T(8,128)(2,1)S(1)} %get-tuple-element.19), channel_id=1, source_target_pairs={{0,6},{1,7},{2,4},{3,5},{4,2},{5,3},{6,0},{7,1},{8,14},{9,15},{10,... | collective-permute-start | bytes 368648 | tf_op jit(solution)/shard_map/ppermute | solution.py:280
  20.0 11.0 %collective-permute-start.2 = (bf16[96,640]{1,0:T(8,128)(2,1)S(1)}, bf16[96,640]{1,0:T(8,128)(2,1)S(1)}, u32[]{:S(2)}, u32[]{:S(2)}) collective-permute-start(bf16[96,640]{1,0:T(8,128)(2,1)S(1)} %get-tuple-element.16.refs_0_), channel_id=1, source_target_pairs={{0,1},{1,0},{2,3},{3,2},{4,5},{5,4},{6,7},{7,6},{8,9},{9,8},{10,11... | collective-permute-start | bytes 368648 | tf_op jit(solution)/shard_map/ppermute | solution.py:283
  22.0 9.0 %collective-permute-start.4 = (bf16[96,640]{1,0:T(8,128)(2,1)S(1)}, bf16[96,640]{1,0:T(8,128)(2,1)S(1)}, u32[]{:S(2)}, u32[]{:S(2)}) collective-permute-start(bf16[96,640]{1,0:T(8,128)(2,1)S(1)} %collective-permute-done.3.refs_2_), channel_id=1, source_target_pairs={{0,1},{1,0},{2,3},{3,2},{4,5},{5,4},{6,7},{7,6},{8,9},{9,8},{10,11... | collective-permute-start | bytes 368648 | tf_op jit(solution)/shard_map/ppermute | solution.py:283
  23.8 8.1 %collective-permute-start.6 = (bf16[96,640]{1,0:T(8,128)(2,1)S(1)}, bf16[96,640]{1,0:T(8,128)(2,1)S(1)}, u32[]{:S(2)}, u32[]{:S(2)}) collective-permute-start(bf16[96,640]{1,0:T(8,128)(2,1)S(1)} %collective-permute-done.5.refs_4_), channel_id=1, source_target_pairs={{0,1},{1,0},{2,3},{3,2},{4,5},{5,4},{6,7},{7,6},{8,9},{9,8},{10,11... | collective-permute-start | bytes 368648 | tf_op jit(solution)/shard_map/ppermute | solution.py:283
  31.0 1.3 %collective-permute-start.8 = (bf16[96,640]{1,0:T(8,128)(2,1)S(1)}, bf16[96,640]{1,0:T(8,128)(2,1)S(1)}, u32[]{:S(2)}, u32[]{:S(2)}) collective-permute-start(bf16[96,640]{1,0:T(8,128)(2,1)S(1)} %collective-permute-done.7.refs_6_), channel_id=1, source_target_pairs={{0,1},{1,0},{2,3},{3,2},{4,5},{5,4},{6,7},{7,6},{8,9},{9,8},{10,11... | collective-permute-start | bytes 368648 | tf_op jit(solution)/shard_map/ppermute | solution.py:283

commit v2 on v1

--- a/solution.py
+++ b/solution.py
@@ -17,18 +17,19 @@
 BF16 = jnp.bfloat16
 VMEM = pl.BlockSpec(memory_space=pltpu.VMEM)
 SMEM = pl.BlockSpec(memory_space=pltpu.SMEM)
-PARAMS = pltpu.CompilerParams(vmem_limit_bytes=48 * 1024 * 1024)
-
-
-def prepare_kernel(image_ref, inv_var_ref, main_ref, first_ref, last_ref):
-    epochs, _, rows = image_ref.shape
+PARAMS = pltpu.CompilerParams(vmem_limit_bytes=24 * 1024 * 1024)
+
+
+def prepare_kernel(weighted_ref, variance_ref, main_ref, even_ref, odd_ref):
+    epochs, _, rows = weighted_ref.shape
+    even = lax.rem(lax.axis_index("tm"), 2) == 0
     for ep in range(epochs):
-        inv_var = inv_var_ref[ep]
-        for plane, values in ((0, image_ref[ep] * inv_var), (1, inv_var)):
-            turned = values.T.astype(BF16)
-            main_ref[plane, ep] = turned
-            first_ref[plane, ep] = turned[:HALO]
-            last_ref[plane, ep] = turned[rows - HALO :]
+        for plane, ref in ((0, weighted_ref), (1, variance_ref)):
+            turned = ref[ep].astype(F32).T
+            main_ref[plane, ep] = turned.astype(BF16)
+            first, last = turned[:HALO], turned[rows - HALO :]
+            even_ref[plane, ep] = jnp.where(even, last, first).astype(BF16)
+            odd_ref[plane, ep] = jnp.where(even, first, last).astype(BF16)
 
 
 def prepare(image, inv_var):
@@ -41,10 +42,10 @@
         out_specs=[VMEM] * 3,
         compiler_params=PARAMS,
         name="prepare",
-    )(image, inv_var)
-
-
-def band_kernel(psf_ref, band_ref, corner_ref):
+    )((image * inv_var).astype(BF16), inv_var.astype(BF16))
+
+
+def band_kernel(psf_ref, band_ref, *corner_refs):
     psf = psf_ref[...]
     normed = psf / jnp.sum(psf)
     flip = (
@@ -70,38 +71,49 @@
             from_right = jnp.where(below, ring, 0.0).astype(BF16)
             band_ref[plane, at : at + LANES, LANES:] = from_left
             band_ref[plane, at + LANES : at + BLOCK, :LANES] = from_right
-            corner_ref[plane, 0, j * LANES : (j + 1) * LANES] = from_left
-            corner_ref[plane, 1, j * LANES : (j + 1) * LANES] = from_right
-
-
-def band_matrices(psf):
+            for corner_ref in corner_refs:
+                corner_ref[plane, 0, j * LANES : (j + 1) * LANES] = from_left
+                corner_ref[plane, 1, j * LANES : (j + 1) * LANES] = from_right
+
+
+def band_matrices(psf, blocks):
+    shapes = [jax.ShapeDtypeStruct((2, TAPS * BLOCK, BLOCK), BF16)]
+    if blocks > 1:
+        shapes.append(jax.ShapeDtypeStruct((2, 2, TAPS * LANES, LANES), BF16))
     return pl.pallas_call(
         band_kernel,
-        out_shape=(
-            jax.ShapeDtypeStruct((2, TAPS * BLOCK, BLOCK), BF16),
-            jax.ShapeDtypeStruct((2, 2, TAPS * LANES, LANES), BF16),
-        ),
+        out_shape=shapes,
         in_specs=[VMEM],
-        out_specs=[VMEM] * 2,
+        out_specs=[VMEM] * len(shapes),
         compiler_params=PARAMS,
         name="band",
     )(psf)
 
 
-def filter_kernel(chips, where_ref, main_ref, before_ref, after_ref, band_ref, corner_ref, *refs):
+def filter_kernel(chips, where_ref, main_ref, even_ref, odd_ref, band_ref, *refs):
+    blocks = main_ref.shape[3] // BLOCK
+    if blocks > 1:
+        corner_ref, refs = refs[0], refs[1:]
     outs, (tall, lhs, corner_lhs, turned, wide) = refs[:chips], refs[chips:]
     _, epochs, rows, width = main_ref.shape
     out_rows = rows + 2 * MAXSHIFT
+    chip, row_block, height = where_ref[0], where_ref[1], where_ref[2]
+    even = lax.rem(row_block, 2) == 0
     for plane in range(2):
         for ep in range(epochs):
-            tall[plane, ep, :HALO] = before_ref[plane, ep]
             tall[plane, ep, HALO : HALO + rows] = main_ref[plane, ep]
-            tall[plane, ep, HALO + rows :] = after_ref[plane, ep]
-    chip, row_block, height = where_ref[0], where_ref[1], where_ref[2]
+    for is_even, before_ref, after_ref in ((True, odd_ref, even_ref), (False, even_ref, odd_ref)):
+
+        @pl.when(even == is_even)
+        def _():
+            for plane in range(2):
+                for ep in range(epochs):
+                    tall[plane, ep, :HALO] = before_ref[plane, ep]
+                    tall[plane, ep, HALO + rows :] = after_ref[plane, ep]
+
     row = row_block * rows - MAXSHIFT + lax.broadcasted_iota(jnp.int32, (out_rows, BLOCK), 0)
     inside = (row >= 0) & (row < height)
     skip = HALO - MAXSHIFT - RADIUS
-    blocks = width // BLOCK
     for block in range(blocks):
         at = block * BLOCK
         filtered = []
@@ -155,7 +167,7 @@
         outs[k][...] = wide[pl.ds(start, span + 2 * MAXSHIFT), :]
 
 
-def filter_epochs(where, main, before, after, band, corner, chips):
+def filter_epochs(where, main, even, odd, bands, chips):
     _, epochs, rows, width = main.shape
     out_rows = rows + 2 * MAXSHIFT
     lanes = (2 * epochs + 1) * LANES
@@ -163,7 +175,7 @@
     return pl.pallas_call(
         functools.partial(filter_kernel, chips),
         out_shape=(piece,) * chips,
-        in_specs=[SMEM] + [VMEM] * 5,
+        in_specs=[SMEM] + [VMEM] * (3 + len(bands)),
         out_specs=[VMEM] * chips,
         scratch_shapes=[
             pltpu.VMEM((2, epochs, rows + 2 * HALO, width), BF16),
@@ -174,7 +186,7 @@
         ],
         compiler_params=PARAMS,
         name="filter",
-    )(where, main, before, after, band, corner)
+    )(where, main, even, odd, *bands)
 
 
 def stack_kernel(chips, vels, where_ref, shifts_ref, *refs):
@@ -235,7 +247,7 @@
         return jnp.maximum(top, like), total + jnp.exp(like)
 
     top = jnp.full((cols, LANES), -jnp.inf, F32)
-    top, total = lax.fori_loop(0, vels, visit, (top, jnp.zeros((cols, LANES), F32)))
+    top, total = lax.fori_loop(0, vels, visit, (top, jnp.zeros((cols, LANES), F32)), unroll=4)
     best_ref[...] = top
     score_ref[...] = jnp.log(total / vels)
 
@@ -265,13 +277,13 @@
     where = jnp.stack([place // 2, row_block, rows * row_blocks, place % 2]).astype(jnp.int32)
     table = jnp.transpose(shifts, (0, 2, 1)).reshape(2 * shifts.shape[0], shifts.shape[1])
 
-    main, first, last = prepare(image, inv_var)
-    up = [(i, i + 1) for i in range(row_blocks - 1)]
-    down = [(j, i) for i, j in up]
-    before = lax.ppermute(last, "tm", up)
-    after = lax.ppermute(first, "tm", down)
-    band, corner = band_matrices(psf)
-    sent = filter_epochs(where, main, before, after, band, corner, chips)
+    main, even, odd = prepare(image, inv_var)
+    evens = [(i, i + 1) for i in range(0, row_blocks - 1, 2)]
+    odds = [(i, i + 1) for i in range(1, row_blocks - 1, 2)]
+    even = lax.ppermute(even, "tm", evens + [(j, i) for i, j in evens])
+    odd = lax.ppermute(odd, "tm", odds + [(j, i) for i, j in odds])
+    bands = band_matrices(psf, width // BLOCK)
+    sent = filter_epochs(where, main, even, odd, bands, chips)
 
     swap = [(i, i ^ 1) for i in range(devices)]
     got = {0: sent[0]}

time: 37.7 us -> 31.4 us (0.83)
  local copies, waits for them, and re-layouts: 4.45 us -> 0.7 us
  starting transfers between devices: 20.8 us -> 17.8 us
  Pallas kernels: 10 us -> 7.32 us
  waiting for transfers between devices: 1.34 us -> 3.5 us
  other arithmetic: 0.08 us -> 1.23 us
    unnamed x10 -> x4, local copies, waits for them, and re-layouts: 4.45 us -> 0.7 us
    ppermute x2, starting transfers between devices: 6.18 us -> 3.18 us  [the longest x1 1.91 us: on_device(): odd = lax.ppermute(odd, 'tm', odds + [(j, i) for i, j in odds])]
    ppermute x2, waiting for transfers between devices: 0.01 us -> 2.17 us  [the longest x1 2.17 us: on_device(): odd = lax.ppermute(odd, 'tm', odds + [(j, i) for i, j in odds])]
    pallas_call x1, Pallas kernels: 3.85 us -> 2.29 us  [filter_epochs(): pl.pallas_call(functools.partial(filter_kernel, chips), out_shape=(piece,...]
    convert_element_type x0 -> x1, other arithmetic: none -> 1.16 us  [prepare(): inv_var.astype(BF16)]
    pallas_call x1, Pallas kernels: 5.11 us -> 4.07 us  [stack_epochs(): pl.pallas_call(functools.partial(stack_kernel, chips, vels), out_shape=(o...]
  transfers between devices with their start and end apart: 9 -> 9, of which waited for: 2 -> 3; matrix products, arithmetic and copies ran while one was open for 0% -> 0% of each run, Pallas kernels for 3% -> 3%
where the time goes in v2:
time: 31.4 us; the launch traced here: 31.2 us
  starting transfers between devices  17.8 us (57%)
  Pallas kernels  7.32 us (23%)
  waiting for transfers between devices  3.5 us (11%)
  other arithmetic  1.23 us (4%)
  between operations  0.71 us (2%)
  local copies, waits for them, and re-layouts  0.7 us (2%)
    ppermute x4, starting transfers between devices, on_device(): pieces += [got[k], lax.ppermute(got[k], 'space', swap)]  10.9 us
    pallas_call x1, Pallas kernels, stack_epochs(): pl.pallas_call(functools.partial(stack_kernel, chips, vels), out_shape=(o...  4.07 us
    ppermute x3, starting transfers between devices, on_device(): got[k] = lax.ppermute(sent[k], 'space', pairs)  3.67 us
    pallas_call x1, Pallas kernels, filter_epochs(): pl.pallas_call(functools.partial(filter_kernel, chips), out_shape=(piece,...  2.29 us
    ppermute x1, waiting for transfers between devices, on_device(): odd = lax.ppermute(odd, 'tm', odds + [(j, i) for i, j in odds])  2.17 us
    ppermute x1, starting transfers between devices, on_device(): odd = lax.ppermute(odd, 'tm', odds + [(j, i) for i, j in odds])  1.91 us
    ppermute x4, waiting for transfers between devices, on_device(): pieces += [got[k], lax.ppermute(got[k], 'space', swap)]  1.32 us
    ppermute x1, starting transfers between devices, on_device(): even = lax.ppermute(even, 'tm', evens + [(j, i) for i, j in evens])  1.28 us
  transfers between devices with their start and end apart: 9, of which 3 were waited for; matrix products, arithmetic and copies ran while one was open for 0% of the time, Pallas kernels for 3%

profile of v2, /device:TPU:5, one launch (start us, length us, event | category | flops | bytes accessed | tf_op | source)
XLA Modules:
  0.0 31.2 jit_solution(17278151656883146636)
XLA Ops:
  0.6 1.2 %fusion = (bf16[2,256,128]{2,1,0:T(8,128)(2,1)S(1)}, bf16[2,256,128]{2,1,0:T(8,128)(2,1)S(1)}) fusion(f32[2,256,128]{2,1,0:T(8,128)} %param.5, f32[2,256,128]{2,1,0:T(8,128)} %param.4), kind=kLoop, calls=%fused_computation.2 | loop fusion | flops 196608 | bytes 786432 | tf_op jit(solution)/shard_map/convert_element_type | solution.py:45
  1.8 0.1 prepare.1
  1.9 1.3 %collective-permute-start = (bf16[2,2,24,256]{3,2,1,0:T(8,128)(2,1)S(1)}, bf16[2,2,24,256]{3,2,1,0:T(8,128)(2,1)S(1)}, u32[]{:S(2)}, u32[]{:S(2)}) collective-permute-start(bf16[2,2,24,256]{3,2,1,0:T(8,128)(2,1)S(1)} %get-tuple-element.10), channel_id=1, source_target_pairs={{0,8},{16,24},{8,0},{24,16},{1,9},{17,25},{9,1},{25,17},{2,10},{18... | collective-permute-start | bytes 147464 | tf_op jit(solution)/shard_map/ppermute | solution.py:283
  3.2 1.9 %collective-permute-start.1 = (bf16[2,2,24,256]{3,2,1,0:T(8,128)(2,1)S(1)}, bf16[2,2,24,256]{3,2,1,0:T(8,128)(2,1)S(1)}, u32[]{:S(2)}, u32[]{:S(2)}) collective-permute-start(bf16[2,2,24,256]{3,2,1,0:T(8,128)(2,1)S(1)} %get-tuple-element.11), channel_id=1, source_target_pairs={{8,16},{16,8},{9,17},{17,9},{10,18},{18,10},{11,19},{19,11},{12,20... | collective-permute-start | bytes 147464 | tf_op jit(solution)/shard_map/ppermute | solution.py:284
  5.1 0.1 pad_add_fusion.where_ref
  5.2 0.0 copy-start.1
  5.2 0.7 %copy-done.1 = f32[15,15]{1,0:T(8,128)S(1)} copy-done((f32[15,15]{1,0:T(8,128)S(1)}, f32[15,15]{1,0:T(8,128)}, u32[]{:S(2)}) %copy-start.1) | copy-done | bytes 924
  5.9 0.0 copy-start
  5.9 0.8 %band.1.band_ref = bf16[2,3840,256]{2,1,0:T(8,128)(2,1)S(1)} custom-call(f32[15,15]{1,0:T(8,128)S(1)} %copy-done.1), custom_call_target="tpu_custom_call" | custom-call | tf_op jit(solution)/shard_map/band/pallas_call | solution.py:83
  6.8 0.0 collective-permute-done.even_ref
  6.8 2.2 %collective-permute-done.1.odd_ref = bf16[2,2,24,256]{3,2,1,0:T(8,128)(2,1)S(1)} collective-permute-done((bf16[2,2,24,256]{3,2,1,0:T(8,128)(2,1)S(1)}, bf16[2,2,24,256]{3,2,1,0:T(8,128)(2,1)S(1)}, u32[]{:S(2)}, u32[]{:S(2)}) %collective-permute-start.1) | collective-permute-done | bytes 49184 | tf_op jit(solution)/shard_map/ppermute | solution.py:284
  8.9 2.3 %filter.1 = (bf16[96,640]{1,0:T(8,128)(2,1)S(1)}, bf16[96,640]{1,0:T(8,128)(2,1)S(1)}, bf16[96,640]{1,0:T(8,128)(2,1)S(1)}, bf16[96,640]{1,0:T(8,128)(2,1)S(1)}) custom-call(s32[4]{0:T(128)S(1)} %pad_add_fusion.where_ref, bf16[2,2,128,256]{3,2,1,0:T(8,128)(2,1)S(1)} %get-tuple-element.9.main_ref, bf16[2,2,24,256]{3,2,1,0:T(8,128)(2,1)S(1)} %collective-permute-done.even_ref, ...), custom_call_target="tpu_custom_call" | custom-call | tf_op jit(solution)/shard_map/filter/pallas_call | solution.py:175
  11.2 1.4 %collective-permute-start.3 = (bf16[96,640]{1,0:T(8,128)(2,1)S(1)}, bf16[96,640]{1,0:T(8,128)(2,1)S(1)}, u32[]{:S(2)}, u32[]{:S(2)}) collective-permute-start(bf16[96,640]{1,0:T(8,128)(2,1)S(1)} %get-tuple-element.13), channel_id=1, source_target_pairs={{0,2},{1,3},{2,0},{3,1},{4,6},{5,7},{6,4},{7,5},{8,10},{9,11},{10,... | collective-permute-start | bytes 368648 | tf_op jit(solution)/shard_map/ppermute | solution.py:292
  12.6 2.3 %collective-permute-start.5 = (bf16[96,640]{1,0:T(8,128)(2,1)S(1)}, bf16[96,640]{1,0:T(8,128)(2,1)S(1)}, u32[]{:S(2)}, u32[]{:S(2)}) collective-permute-start(bf16[96,640]{1,0:T(8,128)(2,1)S(1)} %get-tuple-element.14), channel_id=1, source_target_pairs={{0,4},{1,5},{2,6},{3,7},{4,0},{5,1},{6,2},{7,3},{8,12},{9,13},{10,... | collective-permute-start | bytes 368648 | tf_op jit(solution)/shard_map/ppermute | solution.py:292
  14.9 0.0 collective-permute-start.7
  14.9 2.9 %collective-permute-start.2 = (bf16[96,640]{1,0:T(8,128)(2,1)S(1)}, bf16[96,640]{1,0:T(8,128)(2,1)S(1)}, u32[]{:S(2)}, u32[]{:S(2)}) collective-permute-start(bf16[96,640]{1,0:T(8,128)(2,1)S(1)} %get-tuple-element.12.refs_0_), channel_id=1, source_target_pairs={{0,1},{1,0},{2,3},{3,2},{4,5},{5,4},{6,7},{7,6},{8,9},{9,8},{10,11... | collective-permute-start | bytes 368648 | tf_op jit(solution)/shard_map/ppermute | solution.py:295
  17.8 0.0 collective-permute-done.3.refs_2_
  17.8 1.4 %collective-permute-start.4 = (bf16[96,640]{1,0:T(8,128)(2,1)S(1)}, bf16[96,640]{1,0:T(8,128)(2,1)S(1)}, u32[]{:S(2)}, u32[]{:S(2)}) collective-permute-start(bf16[96,640]{1,0:T(8,128)(2,1)S(1)} %collective-permute-done.3.refs_2_), channel_id=1, source_target_pairs={{0,1},{1,0},{2,3},{3,2},{4,5},{5,4},{6,7},{7,6},{8,9},{9,8},{10,11... | collective-permute-start | bytes 368648 | tf_op jit(solution)/shard_map/ppermute | solution.py:295
  19.2 0.0 collective-permute-done.5.refs_4_
  19.2 6.6 %collective-permute-start.6 = (bf16[96,640]{1,0:T(8,128)(2,1)S(1)}, bf16[96,640]{1,0:T(8,128)(2,1)S(1)}, u32[]{:S(2)}, u32[]{:S(2)}) collective-permute-start(bf16[96,640]{1,0:T(8,128)(2,1)S(1)} %collective-permute-done.5.refs_4_), channel_id=1, source_target_pairs={{0,1},{1,0},{2,3},{3,2},{4,5},{5,4},{6,7},{7,6},{8,9},{9,8},{10,11... | collective-permute-start | bytes 368648 | tf_op jit(solution)/shard_map/ppermute | solution.py:295
  25.8 0.0 collective-permute-done.7.refs_6_
  25.8 0.0 collective-permute-start.8
  25.8 0.0 collective-permute-done.2.refs_1_
  25.8 0.0 collective-permute-done.4.refs_3_
  25.8 1.0 %collective-permute-done.6.refs_5_ = bf16[96,640]{1,0:T(8,128)(2,1)S(1)} collective-permute-done((bf16[96,640]{1,0:T(8,128)(2,1)S(1)}, bf16[96,640]{1,0:T(8,128)(2,1)S(1)}, u32[]{:S(2)}, u32[]{:S(2)}) %collective-permute-start.6) | collective-permute-done | bytes 122912 | tf_op jit(solution)/shard_map/ppermute | solution.py:295
  26.8 0.4 %collective-permute-done.8.refs_7_ = bf16[96,640]{1,0:T(8,128)(2,1)S(1)} collective-permute-done((bf16[96,640]{1,0:T(8,128)(2,1)S(1)}, bf16[96,640]{1,0:T(8,128)(2,1)S(1)}, u32[]{:S(2)}, u32[]{:S(2)}) %collective-permute-start.8) | collective-permute-done | bytes 122912 | tf_op jit(solution)/shard_map/ppermute | solution.py:295
  27.2 0.0 copy-done
  27.2 4.1 %stack.17 = (f32[32,128]{1,0:T(8,128)}, f32[32,128]{1,0:T(8,128)}) custom-call(s32[4]{0:T(128)S(1)} %pad_add_fusion.where_ref, s32[32,16]{1,0:T(8,128)S(1)} %bitcast.6, bf16[96,640]{1,0:T(8,128)(2,1)S(1)} %get-tuple-element.12.refs_0_, bf16[96,640]{1,0:T(8,128)(2,1)S(1)} %collective-permute-done.2.refs_1_, ...), custom_call_target="tpu_custom_call" | custom-call | tf_op jit(solution)/shard_map/stack/pallas_call | solution.py:260
Async XLA Ops:
  1.9 4.8 %collective-permute-start = (bf16[2,2,24,256]{3,2,1,0:T(8,128)(2,1)S(1)}, bf16[2,2,24,256]{3,2,1,0:T(8,128)(2,1)S(1)}, u32[]{:S(2)}, u32[]{:S(2)}) collective-permute-start(bf16[2,2,24,256]{3,2,1,0:T(8,128)(2,1)S(1)} %get-tuple-element.10), channel_id=1, source_target_pairs={{0,8},{16,24},{8,0},{24,16},{1,9},{17,25},{9,1},{25,17},{2,10},{18... | collective-permute-start | bytes 147464 | tf_op jit(solution)/shard_map/ppermute | solution.py:283
  3.2 5.7 %collective-permute-start.1 = (bf16[2,2,24,256]{3,2,1,0:T(8,128)(2,1)S(1)}, bf16[2,2,24,256]{3,2,1,0:T(8,128)(2,1)S(1)}, u32[]{:S(2)}, u32[]{:S(2)}) collective-permute-start(bf16[2,2,24,256]{3,2,1,0:T(8,128)(2,1)S(1)} %get-tuple-element.11), channel_id=1, source_target_pairs={{8,16},{16,8},{9,17},{17,9},{10,18},{18,10},{11,19},{19,11},{12,20... | collective-permute-start | bytes 147464 | tf_op jit(solution)/shard_map/ppermute | solution.py:284
  5.2 0.7 %copy-start.1 = (f32[15,15]{1,0:T(8,128)S(1)}, f32[15,15]{1,0:T(8,128)}, u32[]{:S(2)}) copy-start(f32[15,15]{1,0:T(8,128)} %psf_ref.1) | copy-start | bytes 2704
  5.9 21.2 %copy-start = (s32[16,16,2]{1,2,0:T(2,128)S(1)}, s32[16,16,2]{1,2,0:T(2,128)}, u32[]{:S(2)}) copy-start(s32[16,16,2]{1,2,0:T(2,128)} %param.7) | copy-start | bytes 6148
  11.2 6.6 %collective-permute-start.3 = (bf16[96,640]{1,0:T(8,128)(2,1)S(1)}, bf16[96,640]{1,0:T(8,128)(2,1)S(1)}, u32[]{:S(2)}, u32[]{:S(2)}) collective-permute-start(bf16[96,640]{1,0:T(8,128)(2,1)S(1)} %get-tuple-element.13), channel_id=1, source_target_pairs={{0,2},{1,3},{2,0},{3,1},{4,6},{5,7},{6,4},{7,5},{8,10},{9,11},{10,... | collective-permute-start | bytes 368648 | tf_op jit(solution)/shard_map/ppermute | solution.py:292
  12.6 6.6 %collective-permute-start.5 = (bf16[96,640]{1,0:T(8,128)(2,1)S(1)}, bf16[96,640]{1,0:T(8,128)(2,1)S(1)}, u32[]{:S(2)}, u32[]{:S(2)}) collective-permute-start(bf16[96,640]{1,0:T(8,128)(2,1)S(1)} %get-tuple-element.14), channel_id=1, source_target_pairs={{0,4},{1,5},{2,6},{3,7},{4,0},{5,1},{6,2},{7,3},{8,12},{9,13},{10,... | collective-permute-start | bytes 368648 | tf_op jit(solution)/shard_map/ppermute | solution.py:292
  14.9 10.9 %collective-permute-start.7 = (bf16[96,640]{1,0:T(8,128)(2,1)S(1)}, bf16[96,640]{1,0:T(8,128)(2,1)S(1)}, u32[]{:S(2)}, u32[]{:S(2)}) collective-permute-start(bf16[96,640]{1,0:T(8,128)(2,1)S(1)} %get-tuple-element.15), channel_id=1, source_target_pairs={{0,6},{1,7},{2,4},{3,5},{4,2},{5,3},{6,0},{7,1},{8,14},{9,15},{10,... | collective-permute-start | bytes 368648 | tf_op jit(solution)/shard_map/ppermute | solution.py:292
  14.9 10.9 %collective-permute-start.2 = (bf16[96,640]{1,0:T(8,128)(2,1)S(1)}, bf16[96,640]{1,0:T(8,128)(2,1)S(1)}, u32[]{:S(2)}, u32[]{:S(2)}) collective-permute-start(bf16[96,640]{1,0:T(8,128)(2,1)S(1)} %get-tuple-element.12.refs_0_), channel_id=1, source_target_pairs={{0,1},{1,0},{2,3},{3,2},{4,5},{5,4},{6,7},{7,6},{8,9},{9,8},{10,11... | collective-permute-start | bytes 368648 | tf_op jit(solution)/shard_map/ppermute | solution.py:295
  17.8 8.0 %collective-permute-start.4 = (bf16[96,640]{1,0:T(8,128)(2,1)S(1)}, bf16[96,640]{1,0:T(8,128)(2,1)S(1)}, u32[]{:S(2)}, u32[]{:S(2)}) collective-permute-start(bf16[96,640]{1,0:T(8,128)(2,1)S(1)} %collective-permute-done.3.refs_2_), channel_id=1, source_target_pairs={{0,1},{1,0},{2,3},{3,2},{4,5},{5,4},{6,7},{7,6},{8,9},{9,8},{10,11... | collective-permute-start | bytes 368648 | tf_op jit(solution)/shard_map/ppermute | solution.py:295
  19.2 7.6 %collective-permute-start.6 = (bf16[96,640]{1,0:T(8,128)(2,1)S(1)}, bf16[96,640]{1,0:T(8,128)(2,1)S(1)}, u32[]{:S(2)}, u32[]{:S(2)}) collective-permute-start(bf16[96,640]{1,0:T(8,128)(2,1)S(1)} %collective-permute-done.5.refs_4_), channel_id=1, source_target_pairs={{0,1},{1,0},{2,3},{3,2},{4,5},{5,4},{6,7},{7,6},{8,9},{9,8},{10,11... | collective-permute-start | bytes 368648 | tf_op jit(solution)/shard_map/ppermute | solution.py:295
  25.8 1.3 %collective-permute-start.8 = (bf16[96,640]{1,0:T(8,128)(2,1)S(1)}, bf16[96,640]{1,0:T(8,128)(2,1)S(1)}, u32[]{:S(2)}, u32[]{:S(2)}) collective-permute-start(bf16[96,640]{1,0:T(8,128)(2,1)S(1)} %collective-permute-done.7.refs_6_), channel_id=1, source_target_pairs={{0,1},{1,0},{2,3},{3,2},{4,5},{5,4},{6,7},{7,6},{8,9},{9,8},{10,11... | collective-permute-start | bytes 368648 | tf_op jit(solution)/shard_map/ppermute | solution.py:295

commit v3 on v2

--- a/solution.py
+++ b/solution.py
@@ -90,14 +90,16 @@
     )(psf)
 
 
-def filter_kernel(chips, where_ref, main_ref, even_ref, odd_ref, band_ref, *refs):
+def filter_kernel(chips, main_ref, even_ref, odd_ref, band_ref, *refs):
     blocks = main_ref.shape[3] // BLOCK
     if blocks > 1:
         corner_ref, refs = refs[0], refs[1:]
     outs, (tall, lhs, corner_lhs, turned, wide) = refs[:chips], refs[chips:]
     _, epochs, rows, width = main_ref.shape
     out_rows = rows + 2 * MAXSHIFT
-    chip, row_block, height = where_ref[0], where_ref[1], where_ref[2]
+    place, row_block = lax.axis_index("space"), lax.axis_index("tm")
+    chip, core = lax.div(place, 2), lax.rem(place, 2)
+    height = rows * lax.axis_size("tm")
     even = lax.rem(row_block, 2) == 0
     for plane in range(2):
         for ep in range(epochs):
@@ -161,13 +163,18 @@
     wide[:MAXSHIFT] = edge
     wide[MAXSHIFT + width :] = edge
     span = width // chips
+    cols = span // 2
     for k in range(chips):
         other = jnp.bitwise_xor(chip, k)
-        start = pl.multiple_of(other * span, span)
-        outs[k][...] = wide[pl.ds(start, span + 2 * MAXSHIFT), :]
-
-
-def filter_epochs(where, main, even, odd, bands, chips):
+        start = other * span
+        for third in range(3):
+            rows_from = start + lax.rem(third + 2 * core, 3) * cols
+            outs[k][third * cols : (third + 1) * cols] = wide[
+                pl.ds(pl.multiple_of(rows_from, cols), cols), :
+            ]
+
+
+def filter_epochs(main, even, odd, bands, chips):
     _, epochs, rows, width = main.shape
     out_rows = rows + 2 * MAXSHIFT
     lanes = (2 * epochs + 1) * LANES
@@ -175,7 +182,7 @@
     return pl.pallas_call(
         functools.partial(filter_kernel, chips),
         out_shape=(piece,) * chips,
-        in_specs=[SMEM] + [VMEM] * (3 + len(bands)),
+        in_specs=[VMEM] * (3 + len(bands)),
         out_specs=[VMEM] * chips,
         scratch_shapes=[
             pltpu.VMEM((2, epochs, rows + 2 * HALO, width), BF16),
@@ -186,30 +193,32 @@
         ],
         compiler_params=PARAMS,
         name="filter",
-    )(where, main, even, odd, *bands)
-
-
-def stack_kernel(chips, vels, where_ref, shifts_ref, *refs):
-    pieces, (best_ref, score_ref), (frames,) = refs[: 2 * chips], refs[2 * chips : -1], refs[-1:]
-    chip, core = where_ref[0], where_ref[3]
-    cols, rows = best_ref.shape
+    )(main, even, odd, *bands)
+
+
+def stack_kernel(members, vels, first, final, shifts_ref, *refs):
+    count = 2 * len(members)
+    pieces, refs, frames = refs[:count], refs[count:-1], refs[-1]
+    if not first:
+        start_ref, refs = refs[0], refs[1:]
+    place = lax.axis_index("space")
+    chip, core = lax.div(place, 2), lax.rem(place, 2)
+    cols = refs[0].shape[-2]
     window = cols + 2 * MAXSHIFT
     parts = pieces[0].shape[1] // LANES
     epochs = (parts - 1) // 2
-    start = pl.multiple_of(core * cols, cols)
-    for slot in range(2 * chips):
-        for part in range(parts):
-            base = (slot * parts + part) * window
-            frames[base : base + window] = pieces[slot][
-                pl.ds(start, window), part * LANES : (part + 1) * LANES
-            ].astype(F32)
+    for slot in range(count):
+        for half in range(2):
+            own = 2 * cols * core if half == 0 else cols * (1 - core)
+            start = pl.multiple_of(own, cols) if slot % 2 == 0 else half * cols
+            for part in range(parts):
+                base = (slot * parts + part) * window + half * cols
+                frames[base : base + cols] = pieces[slot][
+                    pl.ds(start, cols), part * LANES : (part + 1) * LANES
+                ].astype(F32)
     lane = lax.broadcasted_iota(jnp.int32, (cols, LANES), 1)
 
-    def add_slot(slot, v, upper, lower):
-        if isinstance(slot, int):
-            k, flip = slot // 2, slot % 2
-        else:
-            k, flip = lax.div(slot, 2), lax.rem(slot, 2)
+    def add_slot(slot, k, flip, v, upper, lower):
         owner = 2 * jnp.bitwise_xor(chip, k) + jnp.bitwise_xor(core, flip)
         for ep in range(epochs):
             epoch = owner * epochs + ep
@@ -221,51 +230,63 @@
             for plane, total in ((0, upper), (1, lower)):
                 part = 2 * ep + plane
                 turn = 2 * MAXSHIFT * part
-                place = lane if turn == 0 else lax.rem(lane + (LANES - turn), LANES)
+                spot = lane if turn == 0 else lax.rem(lane + (LANES - turn), LANES)
                 held = frames[pl.ds(base + part * window, cols), :]
-                merged = jnp.where(place < down, extra, held)
+                merged = jnp.where(spot < down, extra, held)
                 sums.append(total + pltpu.roll(merged, lax.rem(2 * LANES - turn - down, LANES), 1))
             upper, lower = sums
         return upper, lower
 
-    def visit(v, carry):
-        top, total = carry
-        upper = jnp.zeros((cols, LANES), F32)
-        lower = jnp.zeros((cols, LANES), F32)
-        group = 8
-        if 2 * chips <= group:
-            for slot in range(2 * chips):
-                upper, lower = add_slot(slot, v, upper, lower)
+    def add_all(v):
+        if first:
+            sums = (jnp.zeros((cols, LANES), F32), jnp.zeros((cols, LANES), F32))
         else:
-            def some(g, sums):
-                for s in range(group):
-                    sums = add_slot(g * group + s, v, *sums)
-                return sums
-
-            upper, lower = lax.fori_loop(0, 2 * chips // group, some, (upper, lower))
-        like = upper * lax.rsqrt(jnp.maximum(lower, 0.02))
-        return jnp.maximum(top, like), total + jnp.exp(like)
-
-    top = jnp.full((cols, LANES), -jnp.inf, F32)
-    top, total = lax.fori_loop(0, vels, visit, (top, jnp.zeros((cols, LANES), F32)), unroll=4)
-    best_ref[...] = top
-    score_ref[...] = jnp.log(total / vels)
-
-
-def stack_epochs(where, shifts, pieces, cols, rows):
+            sums = (start_ref[v, 0], start_ref[v, 1])
+        for i, k in enumerate(members):
+            for flip in range(2):
+                sums = add_slot(2 * i + flip, k, flip, v, *sums)
+        return sums
+
+    unroll = vels if len(members) <= 4 else 1
+    if final:
+        best_ref, score_ref = refs
+
+        def visit(v, carry):
+            top, total = carry
+            upper, lower = add_all(v)
+            like = upper * lax.rsqrt(jnp.maximum(lower, 0.02))
+            return jnp.maximum(top, like), total + jnp.exp(like)
+
+        top = jnp.full((cols, LANES), -jnp.inf, F32)
+        top, total = lax.fori_loop(0, vels, visit, (top, jnp.zeros((cols, LANES), F32)), unroll=unroll)
+        best_ref[...] = top
+        score_ref[...] = jnp.log(total / vels)
+    else:
+        (sum_ref,) = refs
+
+        def keep(v, carry):
+            sum_ref[v, 0], sum_ref[v, 1] = add_all(v)
+            return carry
+
+        lax.fori_loop(0, vels, keep, 0, unroll=unroll)
+
+
+def stack_epochs(shifts, members, pieces, sums, final, cols, rows):
     vels = shifts.shape[0] // 2
-    chips = len(pieces) // 2
     parts = pieces[0].shape[1] // LANES
-    out = jax.ShapeDtypeStruct((cols, rows), F32)
+    if final:
+        out_shape = (jax.ShapeDtypeStruct((cols, rows), F32),) * 2
+    else:
+        out_shape = (jax.ShapeDtypeStruct((vels, 2, cols, rows), F32),)
     return pl.pallas_call(
-        functools.partial(stack_kernel, chips, vels),
-        out_shape=(out, out),
-        in_specs=[SMEM] * 2 + [VMEM] * (2 * chips),
-        out_specs=[VMEM] * 2,
-        scratch_shapes=[pltpu.VMEM((2 * chips * parts * (cols + 2 * MAXSHIFT), LANES), F32)],
+        functools.partial(stack_kernel, members, vels, not sums, final),
+        out_shape=out_shape,
+        in_specs=[SMEM] + [VMEM] * (len(pieces) + len(sums)),
+        out_specs=[VMEM] * len(out_shape),
+        scratch_shapes=[pltpu.VMEM((len(pieces) * parts * (cols + 2 * MAXSHIFT), LANES), F32)],
         compiler_params=PARAMS,
-        name="stack",
-    )(where, shifts, *pieces)
+        name="stack_end" if final else "stack_part",
+    )(shifts, *pieces, *sums)
 
 
 def on_device(image, inv_var, psf, shifts):
@@ -273,8 +294,6 @@
     devices = lax.axis_size("space")
     row_blocks = lax.axis_size("tm")
     chips = devices // 2
-    place, row_block = lax.axis_index("space"), lax.axis_index("tm")
-    where = jnp.stack([place // 2, row_block, rows * row_blocks, place % 2]).astype(jnp.int32)
     table = jnp.transpose(shifts, (0, 2, 1)).reshape(2 * shifts.shape[0], shifts.shape[1])
 
     main, even, odd = prepare(image, inv_var)
@@ -283,17 +302,27 @@
     even = lax.ppermute(even, "tm", evens + [(j, i) for i, j in evens])
     odd = lax.ppermute(odd, "tm", odds + [(j, i) for i, j in odds])
     bands = band_matrices(psf, width // BLOCK)
-    sent = filter_epochs(where, main, even, odd, bands, chips)
+    sent = filter_epochs(main, even, odd, bands, chips)
 
     swap = [(i, i ^ 1) for i in range(devices)]
+    cols = width // devices
+
     got = {0: sent[0]}
-    for k in reversed(range(1, chips)):
+    for k in range(1, chips):
         pairs = [(2 * i + c, 2 * (i ^ k) + c) for i in range(chips) for c in range(2)]
         got[k] = lax.ppermute(sent[k], "space", pairs)
-    pieces = []
-    for k in range(chips):
-        pieces += [got[k], lax.ppermute(got[k], "space", swap)]
-    return stack_epochs(where, table, pieces, width // devices, rows)
+    last = chips // 2
+    first = tuple(k for k in reversed(range(chips)) if k not in (1, last))
+    steps = (first, (1,), (last,)) if last > 1 else (first, (last,))
+    sums = ()
+    for step, members in enumerate(steps):
+        if step == 1:
+            got[last], sums = lax.optimization_barrier((got[last], sums))
+        pieces = []
+        for k in members:
+            pieces += [got[k], lax.ppermute(got[k][cols:], "space", swap)]
+        sums = stack_epochs(table, members, pieces, sums, members == (last,), cols, rows)
+    return sums
 
 
 def solution(mesh):

time: 31.4 us -> 29.8 us (0.949); the launches traced: 31.2 us -> 29.2 us
  starting transfers between devices: 17.8 us -> 15.8 us
  Pallas kernels: 7.32 us -> 8.28 us
  waiting for transfers between devices: 3.5 us -> 2.55 us
    ppermute x4, starting transfers between devices: 10.9 us -> 8.68 us  [on_device(): pieces += [got[k], lax.ppermute(got[k][cols:], 'space', swap)]]
    pallas_call x1 -> x3, Pallas kernels: 4.07 us -> 5.57 us  [stack_epochs(): pl.pallas_call(functools.partial(stack_kernel, members, vels, not sums, f...]
    ppermute x4, waiting for transfers between devices: 1.32 us -> 0.01 us  [on_device(): pieces += [got[k], lax.ppermute(got[k][cols:], 'space', swap)]]
    pallas_call x1, Pallas kernels: 2.29 us -> 1.75 us  [filter_epochs(): pl.pallas_call(functools.partial(filter_kernel, chips), out_shape=(piece,...]
  transfers between devices with their start and end apart: 9 -> 9, of which waited for: 3 -> 2; matrix products, arithmetic and copies ran while one was open for 0% -> 0% of each run, Pallas kernels for 3% -> 15%
where the time goes in v3:
time: 29.8 us; the launch traced here: 29.2 us
  starting transfers between devices  15.8 us (53%)
  Pallas kernels  8.28 us (28%)
  waiting for transfers between devices  2.55 us (9%)
  other arithmetic  1.16 us (4%)
  local copies, waits for them, and re-layouts  0.73 us (2%)
  between operations  0.72 us (2%)
    ppermute x4, starting transfers between devices, on_device(): pieces += [got[k], lax.ppermute(got[k][cols:], 'space', swap)]  8.68 us
    pallas_call x3, Pallas kernels, stack_epochs(): pl.pallas_call(functools.partial(stack_kernel, members, vels, not sums, f...  5.57 us
    ppermute x3, starting transfers between devices, on_device(): got[k] = lax.ppermute(sent[k], 'space', pairs)  3.75 us
    ppermute x1, waiting for transfers between devices, on_device(): odd = lax.ppermute(odd, 'tm', odds + [(j, i) for i, j in odds])  2.26 us
    ppermute x1, starting transfers between devices, on_device(): odd = lax.ppermute(odd, 'tm', odds + [(j, i) for i, j in odds])  2.04 us
    pallas_call x1, Pallas kernels, filter_epochs(): pl.pallas_call(functools.partial(filter_kernel, chips), out_shape=(piece,...  1.75 us
    ppermute x1, starting transfers between devices, on_device(): even = lax.ppermute(even, 'tm', evens + [(j, i) for i, j in evens])  1.28 us
    convert_element_type x1, other arithmetic, prepare(): inv_var.astype(BF16)  1.16 us
  transfers between devices with their start and end apart: 9, of which 2 were waited for; matrix products, arithmetic and copies ran while one was open for 0% of the time, Pallas kernels for 15%

profile of v3, /device:TPU:5, one launch (start us, length us, event | category | flops | bytes accessed | tf_op | source)
XLA Modules:
  0.0 29.2 jit_solution(9479756358448971386)
XLA Ops:
  0.6 1.2 %fusion = (bf16[2,256,128]{2,1,0:T(8,128)(2,1)S(1)}, bf16[2,256,128]{2,1,0:T(8,128)(2,1)S(1)}) fusion(f32[2,256,128]{2,1,0:T(8,128)} %param.5, f32[2,256,128]{2,1,0:T(8,128)} %param.4), kind=kLoop, calls=%fused_computation.1 | loop fusion | flops 196608 | bytes 786432 | tf_op jit(solution)/shard_map/convert_element_type | solution.py:45
  1.8 0.1 prepare.1
  1.9 1.3 %collective-permute-start = (bf16[2,2,24,256]{3,2,1,0:T(8,128)(2,1)S(1)}, bf16[2,2,24,256]{3,2,1,0:T(8,128)(2,1)S(1)}, u32[]{:S(2)}, u32[]{:S(2)}) collective-permute-start(bf16[2,2,24,256]{3,2,1,0:T(8,128)(2,1)S(1)} %get-tuple-element.12), channel_id=1, source_target_pairs={{0,8},{16,24},{8,0},{24,16},{1,9},{17,25},{9,1},{25,17},{2,10},{18... | collective-permute-start | bytes 147464 | tf_op jit(solution)/shard_map/ppermute | solution.py:302
  3.2 0.0 copy-start
  3.2 2.0 %collective-permute-start.1 = (bf16[2,2,24,256]{3,2,1,0:T(8,128)(2,1)S(1)}, bf16[2,2,24,256]{3,2,1,0:T(8,128)(2,1)S(1)}, u32[]{:S(2)}, u32[]{:S(2)}) collective-permute-start(bf16[2,2,24,256]{3,2,1,0:T(8,128)(2,1)S(1)} %get-tuple-element.13), channel_id=1, source_target_pairs={{8,16},{16,8},{9,17},{17,9},{10,18},{18,10},{11,19},{19,11},{12,20... | collective-permute-start | bytes 147464 | tf_op jit(solution)/shard_map/ppermute | solution.py:303
  5.3 0.0 copy-start.1
  5.3 0.7 %copy-done.1 = f32[15,15]{1,0:T(8,128)S(1)} copy-done((f32[15,15]{1,0:T(8,128)S(1)}, f32[15,15]{1,0:T(8,128)}, u32[]{:S(2)}) %copy-start.1) | copy-done | bytes 924
  6.0 0.8 %band.1.band_ref = bf16[2,3840,256]{2,1,0:T(8,128)(2,1)S(1)} custom-call(f32[15,15]{1,0:T(8,128)S(1)} %copy-done.1), custom_call_target="tpu_custom_call" | custom-call | tf_op jit(solution)/shard_map/band/pallas_call | solution.py:83
  6.8 0.0 collective-permute-done.even_ref
  6.8 2.3 %collective-permute-done.1.odd_ref = bf16[2,2,24,256]{3,2,1,0:T(8,128)(2,1)S(1)} collective-permute-done((bf16[2,2,24,256]{3,2,1,0:T(8,128)(2,1)S(1)}, bf16[2,2,24,256]{3,2,1,0:T(8,128)(2,1)S(1)}, u32[]{:S(2)}, u32[]{:S(2)}) %collective-permute-start.1) | collective-permute-done | bytes 49184 | tf_op jit(solution)/shard_map/ppermute | solution.py:303
  9.1 1.7 %filter.1 = (bf16[96,640]{1,0:T(8,128)(2,1)S(1)}, bf16[96,640]{1,0:T(8,128)(2,1)S(1)}, bf16[96,640]{1,0:T(8,128)(2,1)S(1)}, bf16[96,640]{1,0:T(8,128)(2,1)S(1)}) custom-call(bf16[2,2,128,256]{3,2,1,0:T(8,128)(2,1)S(1)} %get-tuple-element.11.main_ref, bf16[2,2,24,256]{3,2,1,0:T(8,128)(2,1)S(1)} %collective-permute-done.even_ref, ...), custom_call_target="tpu_custom_call" | custom-call | tf_op jit(solution)/shard_map/filter/pallas_call | solution.py:182
  10.8 3.4 %collective-permute-start.3 = (bf16[96,640]{1,0:T(8,128)(2,1)S(1)}, bf16[96,640]{1,0:T(8,128)(2,1)S(1)}, u32[]{:S(2)}, u32[]{:S(2)}) collective-permute-start(bf16[96,640]{1,0:T(8,128)(2,1)S(1)} %get-tuple-element.15), channel_id=1, source_target_pairs={{0,6},{1,7},{2,4},{3,5},{4,2},{5,3},{6,0},{7,1},{8,14},{9,15},{10,... | collective-permute-start | bytes 368648 | tf_op jit(solution)/shard_map/ppermute | solution.py:313
  14.2 0.0 collective-permute-start.7
  14.2 0.4 %collective-permute-start.2 = (bf16[96,640]{1,0:T(8,128)(2,1)S(1)}, bf16[96,640]{1,0:T(8,128)(2,1)S(1)}, u32[]{:S(2)}, u32[]{:S(2)}) collective-permute-start(bf16[96,640]{1,0:T(8,128)(2,1)S(1)} %get-tuple-element.14), channel_id=1, source_target_pairs={{0,4},{1,5},{2,6},{3,7},{4,0},{5,1},{6,2},{7,3},{8,12},{9,13},{10,... | collective-permute-start | bytes 368648 | tf_op jit(solution)/shard_map/ppermute | solution.py:313
  14.6 2.9 %collective-permute-start.5 = (bf16[64,640]{1,0:T(8,128)(2,1)S(1)}, bf16[64,640]{1,0:T(8,128)(2,1)S(1)}, u32[]{:S(2)}, u32[]{:S(2)}) collective-permute-start(bf16[64,640]{1,0:T(8,128)(2,1)S(1)} %slice.13), channel_id=1, source_target_pairs={{0,1},{1,0},{2,3},{3,2},{4,5},{5,4},{6,7},{7,6},{8,9},{9,8},{10,11... | collective-permute-start | bytes 245768 | tf_op jit(solution)/shard_map/ppermute | solution.py:323
  17.5 0.0 collective-permute-done.3.refs_0_
  17.5 3.0 %collective-permute-start.4 = (bf16[64,640]{1,0:T(8,128)(2,1)S(1)}, bf16[64,640]{1,0:T(8,128)(2,1)S(1)}, u32[]{:S(2)}, u32[]{:S(2)}) collective-permute-start(bf16[64,640]{1,0:T(8,128)(2,1)S(1)} %slice.16), channel_id=1, source_target_pairs={{0,1},{1,0},{2,3},{3,2},{4,5},{5,4},{6,7},{7,6},{8,9},{9,8},{10,11... | collective-permute-start | bytes 245768 | tf_op jit(solution)/shard_map/ppermute | solution.py:323
  20.5 0.0 collective-permute-done.7.refs_0_
  20.5 1.6 %collective-permute-start.8 = (bf16[64,640]{1,0:T(8,128)(2,1)S(1)}, bf16[64,640]{1,0:T(8,128)(2,1)S(1)}, u32[]{:S(2)}, u32[]{:S(2)}) collective-permute-start(bf16[64,640]{1,0:T(8,128)(2,1)S(1)} %slice.17), channel_id=1, source_target_pairs={{0,1},{1,0},{2,3},{3,2},{4,5},{5,4},{6,7},{7,6},{8,9},{9,8},{10,11... | collective-permute-start | bytes 245768 | tf_op jit(solution)/shard_map/ppermute | solution.py:323
  22.1 0.0 collective-permute-done.5.refs_3_
  22.1 0.0 collective-permute-done.4.refs_1_
  22.1 0.0 copy-done
  22.1 2.0 %stack_part.2.refs_2_ = f32[16,2,32,128]{3,2,1,0:T(8,128)S(1)} custom-call(s32[32,16]{1,0:T(8,128)S(1)} %bitcast.3, bf16[96,640]{1,0:T(8,128)(2,1)S(1)} %collective-permute-done.3.refs_0_, bf16[64,640]{1,0:T(8,128)(2,1)S(1)} %collective-permute-done.4.refs_1_, bf16[96,640]{1,0:T(8,128)(2,1)S(1)} %get-tuple-element.16.refs_2_, ...), custom_call_target="tpu_custom_call" | custom-call | tf_op jit(solution)/shard_map/stack_part/pallas_call | solution.py:281
  24.1 0.3 collective-permute-done.2.refs_0_
  24.4 1.2 %collective-permute-start.6 = (bf16[64,640]{1,0:T(8,128)(2,1)S(1)}, bf16[64,640]{1,0:T(8,128)(2,1)S(1)}, u32[]{:S(2)}, u32[]{:S(2)}) collective-permute-start(bf16[64,640]{1,0:T(8,128)(2,1)S(1)} %slice.14), channel_id=1, source_target_pairs={{0,1},{1,0},{2,3},{3,2},{4,5},{5,4},{6,7},{7,6},{8,9},{9,8},{10,11... | collective-permute-start | bytes 245768 | tf_op jit(solution)/shard_map/ppermute | solution.py:323
  25.6 0.0 collective-permute-done.8.refs_1_
  25.6 1.4 %stack_part.3.refs_2_ = f32[16,2,32,128]{3,2,1,0:T(8,128)S(1)} custom-call(s32[32,16]{1,0:T(8,128)S(1)} %bitcast.4, bf16[96,640]{1,0:T(8,128)(2,1)S(1)} %collective-permute-done.7.refs_0_, bf16[64,640]{1,0:T(8,128)(2,1)S(1)} %collective-permute-done.8.refs_1_, f32[16,2,32,128]{3,2,1,0:T(8,128)S(1)} %stack_part.2.refs_2_), custom_call_target="tpu_custom_call" | custom-call | tf_op jit(solution)/shard_map/stack_part/pallas_call | solution.py:281
  27.1 0.0 collective-permute-done.6.refs_1_
  27.1 2.1 %stack_end.1 = (f32[32,128]{1,0:T(8,128)}, f32[32,128]{1,0:T(8,128)}) custom-call(s32[32,16]{1,0:T(8,128)S(1)} %bitcast.5, bf16[96,640]{1,0:T(8,128)(2,1)S(1)} %collective-permute-done.2.refs_0_, bf16[64,640]{1,0:T(8,128)(2,1)S(1)} %collective-permute-done.6.refs_1_, f32[16,2,32,128]{3,2,1,0:T(8,128)S(1)} %stack_part.3.refs_2_), custom_call_target="tpu_custom_call" | custom-call | tf_op jit(solution)/shard_map/stack_end/pallas_call | solution.py:281
  (4 shorter events, 0.0 us)
Async XLA Ops:
  1.9 4.9 %collective-permute-start = (bf16[2,2,24,256]{3,2,1,0:T(8,128)(2,1)S(1)}, bf16[2,2,24,256]{3,2,1,0:T(8,128)(2,1)S(1)}, u32[]{:S(2)}, u32[]{:S(2)}) collective-permute-start(bf16[2,2,24,256]{3,2,1,0:T(8,128)(2,1)S(1)} %get-tuple-element.12), channel_id=1, source_target_pairs={{0,8},{16,24},{8,0},{24,16},{1,9},{17,25},{9,1},{25,17},{2,10},{18... | collective-permute-start | bytes 147464 | tf_op jit(solution)/shard_map/ppermute | solution.py:302
  3.2 18.9 %copy-start = (s32[16,16,2]{1,2,0:T(2,128)S(1)}, s32[16,16,2]{1,2,0:T(2,128)}, u32[]{:S(2)}) copy-start(s32[16,16,2]{1,2,0:T(2,128)} %param.7) | copy-start | bytes 6148
  3.2 5.9 %collective-permute-start.1 = (bf16[2,2,24,256]{3,2,1,0:T(8,128)(2,1)S(1)}, bf16[2,2,24,256]{3,2,1,0:T(8,128)(2,1)S(1)}, u32[]{:S(2)}, u32[]{:S(2)}) collective-permute-start(bf16[2,2,24,256]{3,2,1,0:T(8,128)(2,1)S(1)} %get-tuple-element.13), channel_id=1, source_target_pairs={{8,16},{16,8},{9,17},{17,9},{10,18},{18,10},{11,19},{19,11},{12,20... | collective-permute-start | bytes 147464 | tf_op jit(solution)/shard_map/ppermute | solution.py:303
  5.3 0.7 %copy-start.1 = (f32[15,15]{1,0:T(8,128)S(1)}, f32[15,15]{1,0:T(8,128)}, u32[]{:S(2)}) copy-start(f32[15,15]{1,0:T(8,128)} %psf_ref.1) | copy-start | bytes 2704
  10.8 6.6 %collective-permute-start.3 = (bf16[96,640]{1,0:T(8,128)(2,1)S(1)}, bf16[96,640]{1,0:T(8,128)(2,1)S(1)}, u32[]{:S(2)}, u32[]{:S(2)}) collective-permute-start(bf16[96,640]{1,0:T(8,128)(2,1)S(1)} %get-tuple-element.15), channel_id=1, source_target_pairs={{0,6},{1,7},{2,4},{3,5},{4,2},{5,3},{6,0},{7,1},{8,14},{9,15},{10,... | collective-permute-start | bytes 368648 | tf_op jit(solution)/shard_map/ppermute | solution.py:313
  14.2 6.3 %collective-permute-start.7 = (bf16[96,640]{1,0:T(8,128)(2,1)S(1)}, bf16[96,640]{1,0:T(8,128)(2,1)S(1)}, u32[]{:S(2)}, u32[]{:S(2)}) collective-permute-start(bf16[96,640]{1,0:T(8,128)(2,1)S(1)} %get-tuple-element.18), channel_id=1, source_target_pairs={{0,2},{1,3},{2,0},{3,1},{4,6},{5,7},{6,4},{7,5},{8,10},{9,11},{10,... | collective-permute-start | bytes 368648 | tf_op jit(solution)/shard_map/ppermute | solution.py:313
  14.2 10.1 %collective-permute-start.2 = (bf16[96,640]{1,0:T(8,128)(2,1)S(1)}, bf16[96,640]{1,0:T(8,128)(2,1)S(1)}, u32[]{:S(2)}, u32[]{:S(2)}) collective-permute-start(bf16[96,640]{1,0:T(8,128)(2,1)S(1)} %get-tuple-element.14), channel_id=1, source_target_pairs={{0,4},{1,5},{2,6},{3,7},{4,0},{5,1},{6,2},{7,3},{8,12},{9,13},{10,... | collective-permute-start | bytes 368648 | tf_op jit(solution)/shard_map/ppermute | solution.py:313
  14.6 7.5 %collective-permute-start.5 = (bf16[64,640]{1,0:T(8,128)(2,1)S(1)}, bf16[64,640]{1,0:T(8,128)(2,1)S(1)}, u32[]{:S(2)}, u32[]{:S(2)}) collective-permute-start(bf16[64,640]{1,0:T(8,128)(2,1)S(1)} %slice.13), channel_id=1, source_target_pairs={{0,1},{1,0},{2,3},{3,2},{4,5},{5,4},{6,7},{7,6},{8,9},{9,8},{10,11... | collective-permute-start | bytes 245768 | tf_op jit(solution)/shard_map/ppermute | solution.py:323
  17.5 4.6 %collective-permute-start.4 = (bf16[64,640]{1,0:T(8,128)(2,1)S(1)}, bf16[64,640]{1,0:T(8,128)(2,1)S(1)}, u32[]{:S(2)}, u32[]{:S(2)}) collective-permute-start(bf16[64,640]{1,0:T(8,128)(2,1)S(1)} %slice.16), channel_id=1, source_target_pairs={{0,1},{1,0},{2,3},{3,2},{4,5},{5,4},{6,7},{7,6},{8,9},{9,8},{10,11... | collective-permute-start | bytes 245768 | tf_op jit(solution)/shard_map/ppermute | solution.py:323
  20.5 5.1 %collective-permute-start.8 = (bf16[64,640]{1,0:T(8,128)(2,1)S(1)}, bf16[64,640]{1,0:T(8,128)(2,1)S(1)}, u32[]{:S(2)}, u32[]{:S(2)}) collective-permute-start(bf16[64,640]{1,0:T(8,128)(2,1)S(1)} %slice.17), channel_id=1, source_target_pairs={{0,1},{1,0},{2,3},{3,2},{4,5},{5,4},{6,7},{7,6},{8,9},{9,8},{10,11... | collective-permute-start | bytes 245768 | tf_op jit(solution)/shard_map/ppermute | solution.py:323
  24.4 2.7 %collective-permute-start.6 = (bf16[64,640]{1,0:T(8,128)(2,1)S(1)}, bf16[64,640]{1,0:T(8,128)(2,1)S(1)}, u32[]{:S(2)}, u32[]{:S(2)}) collective-permute-start(bf16[64,640]{1,0:T(8,128)(2,1)S(1)} %slice.14), channel_id=1, source_target_pairs={{0,1},{1,0},{2,3},{3,2},{4,5},{5,4},{6,7},{7,6},{8,9},{9,8},{10,11... | collective-permute-start | bytes 245768 | tf_op jit(solution)/shard_map/ppermute | solution.py:323

commit v4 on v3

--- a/solution.py
+++ b/solution.py
@@ -16,33 +16,53 @@
 F32 = jnp.float32
 BF16 = jnp.bfloat16
 VMEM = pl.BlockSpec(memory_space=pltpu.VMEM)
-SMEM = pl.BlockSpec(memory_space=pltpu.SMEM)
+ANY = pl.BlockSpec(memory_space=pl.ANY)
 PARAMS = pltpu.CompilerParams(vmem_limit_bytes=24 * 1024 * 1024)
 
 
-def prepare_kernel(weighted_ref, variance_ref, main_ref, even_ref, odd_ref):
-    epochs, _, rows = weighted_ref.shape
+def prepare_kernel(image_hbm, inv_var_hbm, psf_hbm, main_ref, even_ref, odd_ref, psf_ref, image, inv_var, sems):
+    epochs, _, rows = image.shape
+    copies = []
+    for ep in range(epochs):
+        for i, (source, target) in enumerate(((image_hbm, image), (inv_var_hbm, inv_var))):
+            copies.append(pltpu.make_async_copy(source.at[ep], target.at[ep], sems.at[ep, i]))
+            copies[-1].start()
+    psf_copy = pltpu.make_async_copy(psf_hbm, psf_ref, sems.at[epochs, 0])
+    psf_copy.start()
     even = lax.rem(lax.axis_index("tm"), 2) == 0
     for ep in range(epochs):
-        for plane, ref in ((0, weighted_ref), (1, variance_ref)):
-            turned = ref[ep].astype(F32).T
+        for copy in copies[2 * ep : 2 * ep + 2]:
+            copy.wait()
+        for plane, values in ((0, image[ep] * inv_var[ep]), (1, inv_var[ep])):
+            turned = values.T
             main_ref[plane, ep] = turned.astype(BF16)
             first, last = turned[:HALO], turned[rows - HALO :]
             even_ref[plane, ep] = jnp.where(even, last, first).astype(BF16)
             odd_ref[plane, ep] = jnp.where(even, first, last).astype(BF16)
-
-
-def prepare(image, inv_var):
+    psf_copy.wait()
+
+
+def prepare(image, inv_var, psf):
     epochs, width, rows = image.shape
     halo = jax.ShapeDtypeStruct((2, epochs, HALO, width), BF16)
     return pl.pallas_call(
         prepare_kernel,
-        out_shape=(jax.ShapeDtypeStruct((2, epochs, rows, width), BF16), halo, halo),
-        in_specs=[VMEM] * 2,
-        out_specs=[VMEM] * 3,
+        out_shape=(
+            jax.ShapeDtypeStruct((2, epochs, rows, width), BF16),
+            halo,
+            halo,
+            jax.ShapeDtypeStruct(psf.shape, F32),
+        ),
+        in_specs=[ANY] * 3,
+        out_specs=[VMEM] * 4,
+        scratch_shapes=[
+            pltpu.VMEM(image.shape, F32),
+            pltpu.VMEM(image.shape, F32),
+            pltpu.SemaphoreType.DMA((epochs + 1, 2)),
+        ],
         compiler_params=PARAMS,
         name="prepare",
-    )((image * inv_var).astype(BF16), inv_var.astype(BF16))
+    )(*(pltpu.with_memory_space_constraint(array, pltpu.HBM) for array in (image, inv_var, psf)))
 
 
 def band_kernel(psf_ref, band_ref, *corner_refs):
@@ -90,120 +110,161 @@
     )(psf)
 
 
-def filter_kernel(chips, main_ref, even_ref, odd_ref, band_ref, *refs):
-    blocks = main_ref.shape[3] // BLOCK
-    if blocks > 1:
-        corner_ref, refs = refs[0], refs[1:]
-    outs, (tall, lhs, corner_lhs, turned, wide) = refs[:chips], refs[chips:]
+def filter_rows(sources, skip, count, at, lhs, corner_lhs, band_ref, corner_ref, plane):
+    width = sources[0].shape[1]
+    for i, source in enumerate(sources):
+        for j in range(TAPS):
+            lhs[i * count : (i + 1) * count, j * BLOCK : (j + 1) * BLOCK] = source[
+                skip + j : skip + j + count, at : at + BLOCK
+            ]
+    total = jnp.dot(lhs[...], band_ref[plane], preferred_element_type=F32)
+    low, high = total[:, :LANES], total[:, LANES:]
+    for side, start in ((0, at - LANES), (1, at + BLOCK)):
+        if start < 0 or start >= width:
+            continue
+        for i, source in enumerate(sources):
+            for j in range(TAPS):
+                corner_lhs[i * count : (i + 1) * count, j * LANES : (j + 1) * LANES] = source[
+                    skip + j : skip + j + count, start : start + LANES
+                ]
+        more = jnp.dot(corner_lhs[...], corner_ref[plane, side], preferred_element_type=F32)
+        low, high = (low + more, high) if side == 0 else (low, high + more)
+    total = jnp.concatenate([low, high], axis=1).astype(BF16).astype(F32)
+    return [total[i * count : (i + 1) * count] for i in range(len(sources))]
+
+
+def weigh(psi, phi):
+    signal = jnp.abs(psi) * lax.rsqrt(jnp.maximum(phi, 0.001))
+    weight = 1.0 / (1.0 + jnp.exp(2.0 * signal - 4.0))
+    return weight * psi, weight * phi
+
+
+def middle_kernel(main_ref, band_ref, *refs):
+    corner_ref, out_ref, (lhs, corner_lhs) = (refs[0] if len(refs) > 3 else None), refs[-3], refs[-2:]
     _, epochs, rows, width = main_ref.shape
-    out_rows = rows + 2 * MAXSHIFT
+    for at in range(0, width, BLOCK):
+        psi, phi = (
+            filter_rows(
+                [main_ref.at[plane, ep] for ep in range(epochs)],
+                MAXSHIFT - RADIUS, rows - 2 * MAXSHIFT, at, lhs, corner_lhs, band_ref, corner_ref, plane,
+            )
+            for plane in range(2)
+        )
+        for ep in range(epochs):
+            out_ref[2 * ep, :, at : at + BLOCK], out_ref[2 * ep + 1, :, at : at + BLOCK] = weigh(psi[ep], phi[ep])
+
+
+def filter_middle(main, bands):
+    _, epochs, rows, width = main.shape
+    inner = rows - 2 * MAXSHIFT
+    return pl.pallas_call(
+        middle_kernel,
+        out_shape=jax.ShapeDtypeStruct((2 * epochs, inner, width), F32),
+        in_specs=[VMEM] * (1 + len(bands)),
+        out_specs=VMEM,
+        scratch_shapes=[
+            pltpu.VMEM((epochs * inner, TAPS * BLOCK), BF16),
+            pltpu.VMEM((epochs * inner, TAPS * LANES), BF16),
+        ],
+        compiler_params=PARAMS,
+        name="middle",
+    )(main, *bands)
+
+
+def border_kernel(chips, main_ref, odd_ref, even_ref, middle_ref, band_ref, *refs):
+    corner_ref, refs = (refs[0], refs[1:]) if main_ref.shape[3] > BLOCK else (None, refs)
+    outs, (ends, lhs, corner_lhs, turned, wide) = refs[:chips], refs[chips:]
+    _, epochs, rows, width = main_ref.shape
     place, row_block = lax.axis_index("space"), lax.axis_index("tm")
     chip, core = lax.div(place, 2), lax.rem(place, 2)
-    height = rows * lax.axis_size("tm")
     even = lax.rem(row_block, 2) == 0
     for plane in range(2):
         for ep in range(epochs):
-            tall[plane, ep, HALO : HALO + rows] = main_ref[plane, ep]
-    for is_even, before_ref, after_ref in ((True, odd_ref, even_ref), (False, even_ref, odd_ref)):
-
-        @pl.when(even == is_even)
-        def _():
+            before = jnp.where(even, odd_ref[plane, ep].astype(F32), even_ref[plane, ep].astype(F32))
+            after = jnp.where(even, even_ref[plane, ep].astype(F32), odd_ref[plane, ep].astype(F32))
+            first = main_ref[plane, ep, :HALO].astype(F32)
+            last = main_ref[plane, ep, rows - HALO :].astype(F32)
+            ends[plane, ep] = jnp.concatenate([before, first], axis=0).astype(BF16)
+            ends[plane, epochs + ep] = jnp.concatenate([last, after], axis=0).astype(BF16)
+    span = 2 * MAXSHIFT
+    row = lax.broadcasted_iota(jnp.int32, (span, BLOCK), 0)
+    above = (row_block > 0) | (row >= MAXSHIFT)
+    below = (row_block < lax.axis_size("tm") - 1) | (row < MAXSHIFT)
+    for at in range(0, width, BLOCK):
+        psi, phi = (
+            filter_rows(
+                [ends.at[plane, i] for i in range(2 * epochs)],
+                HALO - MAXSHIFT - RADIUS, span, at, lhs, corner_lhs, band_ref, corner_ref, plane,
+            )
+            for plane in range(2)
+        )
+        for i in range(2 * epochs):
+            ep, inside = i % epochs, (above if i < epochs else below)
+            values = weigh(psi[i], phi[i])
             for plane in range(2):
-                for ep in range(epochs):
-                    tall[plane, ep, :HALO] = before_ref[plane, ep]
-                    tall[plane, ep, HALO + rows :] = after_ref[plane, ep]
-
-    row = row_block * rows - MAXSHIFT + lax.broadcasted_iota(jnp.int32, (out_rows, BLOCK), 0)
-    inside = (row >= 0) & (row < height)
-    skip = HALO - MAXSHIFT - RADIUS
-    for block in range(blocks):
-        at = block * BLOCK
-        filtered = []
-        for plane in range(2):
-            for ep in range(epochs):
-                for j in range(TAPS):
-                    lhs[ep * out_rows : (ep + 1) * out_rows, j * BLOCK : (j + 1) * BLOCK] = tall[
-                        plane, ep, skip + j : skip + j + out_rows, at : at + BLOCK
-                    ]
-            total = jnp.dot(lhs[...], band_ref[plane], preferred_element_type=F32)
-            low, high = total[:, :LANES], total[:, LANES:]
-            for side, source in ((0, at - LANES), (1, at + BLOCK)):
-                if source < 0 or source >= width:
-                    continue
-                for ep in range(epochs):
-                    for j in range(TAPS):
-                        corner_lhs[ep * out_rows : (ep + 1) * out_rows, j * LANES : (j + 1) * LANES] = tall[
-                            plane, ep, skip + j : skip + j + out_rows, source : source + LANES
-                        ]
-                more = jnp.dot(corner_lhs[...], corner_ref[plane, side], preferred_element_type=F32)
-                low, high = (low + more, high) if side == 0 else (low, high + more)
-            total = jnp.concatenate([low, high], axis=1)
-            parts = []
-            for ep in range(epochs):
-                part = total[ep * out_rows : (ep + 1) * out_rows]
-                parts.append(jnp.where(inside, part.astype(BF16).astype(F32), 0.0))
-            filtered.append(parts)
-        for ep in range(epochs):
-            psi, phi = filtered[0][ep], filtered[1][ep]
-            signal = jnp.abs(psi) * lax.rsqrt(jnp.maximum(phi, 0.001))
-            weight = 1.0 / (1.0 + jnp.exp(2.0 * signal - 4.0))
-            for plane, values in ((0, weight * psi), (1, weight * phi)):
                 slot = 2 * ep + plane
-                turn = (MAXSHIFT * 2 * slot) % rows
-                base = slot * LANES
-                turned[base + turn : base + rows, :] = values[: rows - turn]
-                if turn:
-                    turned[base : base + turn, :] = values[rows - turn : rows]
-                extra = 2 * epochs * LANES + slot * 2 * MAXSHIFT
-                turned[extra : extra + 2 * MAXSHIFT, :] = values[rows:]
+                turn = (span * slot) % rows
+                held = jnp.where(inside, values[plane], 0.0)
+                if i < epochs:
+                    base = slot * LANES
+                    turned[base + turn : base + turn + span, :] = held
+                    inner = middle_ref[slot, :, at : at + BLOCK]
+                    straight = rows - span - turn
+                    if straight:
+                        turned[base + turn + span : base + rows, :] = inner[:straight]
+                    if turn:
+                        turned[base : base + turn, :] = inner[straight:]
+                else:
+                    extra = 2 * epochs * LANES + slot * span
+                    turned[extra : extra + span, :] = held
         for part in range(2 * epochs + 1):
             lanes = slice(part * LANES, (part + 1) * LANES)
             wide[MAXSHIFT + at : MAXSHIFT + at + BLOCK, lanes] = turned[lanes, :].T.astype(BF16)
     edge = jnp.zeros((MAXSHIFT, wide.shape[1]), BF16)
     wide[:MAXSHIFT] = edge
     wide[MAXSHIFT + width :] = edge
-    span = width // chips
-    cols = span // 2
+    cols = width // chips // 2
     for k in range(chips):
-        other = jnp.bitwise_xor(chip, k)
-        start = other * span
+        start = jnp.bitwise_xor(chip, k) * (2 * cols)
         for third in range(3):
             rows_from = start + lax.rem(third + 2 * core, 3) * cols
-            outs[k][third * cols : (third + 1) * cols] = wide[
-                pl.ds(pl.multiple_of(rows_from, cols), cols), :
-            ]
-
-
-def filter_epochs(main, even, odd, bands, chips):
+            outs[k][third * cols : (third + 1) * cols] = wide[pl.ds(pl.multiple_of(rows_from, cols), cols), :]
+
+
+def filter_border(main, odd, even, middle, bands, chips):
     _, epochs, rows, width = main.shape
-    out_rows = rows + 2 * MAXSHIFT
     lanes = (2 * epochs + 1) * LANES
-    piece = jax.ShapeDtypeStruct((width // chips + 2 * MAXSHIFT, lanes), BF16)
+    span = 2 * MAXSHIFT
+    piece = jax.ShapeDtypeStruct((width // chips + span, lanes), BF16)
     return pl.pallas_call(
-        functools.partial(filter_kernel, chips),
+        functools.partial(border_kernel, chips),
         out_shape=(piece,) * chips,
-        in_specs=[VMEM] * (3 + len(bands)),
+        in_specs=[VMEM] * (4 + len(bands)),
         out_specs=[VMEM] * chips,
         scratch_shapes=[
-            pltpu.VMEM((2, epochs, rows + 2 * HALO, width), BF16),
-            pltpu.VMEM((epochs * out_rows, TAPS * BLOCK), BF16),
-            pltpu.VMEM((epochs * out_rows, TAPS * LANES), BF16),
+            pltpu.VMEM((2, 2 * epochs, 2 * HALO, width), BF16),
+            pltpu.VMEM((2 * epochs * span, TAPS * BLOCK), BF16),
+            pltpu.VMEM((2 * epochs * span, TAPS * LANES), BF16),
             pltpu.VMEM((lanes, BLOCK), F32),
-            pltpu.VMEM((width + 2 * MAXSHIFT, lanes), BF16),
+            pltpu.VMEM((width + span, lanes), BF16),
         ],
         compiler_params=PARAMS,
-        name="filter",
-    )(main, even, odd, *bands)
-
-
-def stack_kernel(members, vels, first, final, shifts_ref, *refs):
+        name="border",
+    )(main, odd, even, middle, *bands)
+
+
+def stack_kernel(members, vels, first, final, shifts_hbm, *refs):
     count = 2 * len(members)
-    pieces, refs, frames = refs[:count], refs[count:-1], refs[-1]
+    scratch = 5 if final else 3
+    pieces, refs, scratch = refs[:count], refs[count:-scratch], refs[-scratch:]
+    frames, shifts_ref, sems = scratch[:3]
+    table = pltpu.make_async_copy(shifts_hbm, shifts_ref, sems.at[0])
+    table.start()
     if not first:
         start_ref, refs = refs[0], refs[1:]
     place = lax.axis_index("space")
     chip, core = lax.div(place, 2), lax.rem(place, 2)
-    cols = refs[0].shape[-2]
+    cols = refs[-1].shape[-2]
     window = cols + 2 * MAXSHIFT
     parts = pieces[0].shape[1] // LANES
     epochs = (parts - 1) // 2
@@ -216,6 +277,7 @@
                 frames[base : base + cols] = pieces[slot][
                     pl.ds(start, cols), part * LANES : (part + 1) * LANES
                 ].astype(F32)
+    table.wait()
     lane = lax.broadcasted_iota(jnp.int32, (cols, LANES), 1)
 
     def add_slot(slot, k, flip, v, upper, lower):
@@ -259,8 +321,15 @@
 
         top = jnp.full((cols, LANES), -jnp.inf, F32)
         top, total = lax.fori_loop(0, vels, visit, (top, jnp.zeros((cols, LANES), F32)), unroll=unroll)
-        best_ref[...] = top
-        score_ref[...] = jnp.log(total / vels)
+        best, score = scratch[3:]
+        best[...] = top
+        best_copy = pltpu.make_async_copy(best, best_ref, sems.at[1])
+        best_copy.start()
+        score[...] = jnp.log(total / vels)
+        score_copy = pltpu.make_async_copy(score, score_ref, sems.at[2])
+        score_copy.start()
+        best_copy.wait()
+        score_copy.wait()
     else:
         (sum_ref,) = refs
 
@@ -278,12 +347,19 @@
         out_shape = (jax.ShapeDtypeStruct((cols, rows), F32),) * 2
     else:
         out_shape = (jax.ShapeDtypeStruct((vels, 2, cols, rows), F32),)
+    scratch = [
+        pltpu.VMEM((len(pieces) * parts * (cols + 2 * MAXSHIFT), LANES), F32),
+        pltpu.SMEM(shifts.shape, jnp.int32),
+        pltpu.SemaphoreType.DMA((3,)),
+    ]
+    if final:
+        scratch += [pltpu.VMEM((cols, rows), F32)] * 2
     return pl.pallas_call(
         functools.partial(stack_kernel, members, vels, not sums, final),
         out_shape=out_shape,
-        in_specs=[SMEM] + [VMEM] * (len(pieces) + len(sums)),
-        out_specs=[VMEM] * len(out_shape),
-        scratch_shapes=[pltpu.VMEM((len(pieces) * parts * (cols + 2 * MAXSHIFT), LANES), F32)],
+        in_specs=[ANY] + [VMEM] * (len(pieces) + len(sums)),
+        out_specs=[ANY if final else VMEM] * len(out_shape),
+        scratch_shapes=scratch,
         compiler_params=PARAMS,
         name="stack_end" if final else "stack_part",
     )(shifts, *pieces, *sums)
@@ -296,13 +372,14 @@
     chips = devices // 2
     table = jnp.transpose(shifts, (0, 2, 1)).reshape(2 * shifts.shape[0], shifts.shape[1])
 
-    main, even, odd = prepare(image, inv_var)
+    main, even, odd, psf = prepare(image, inv_var, psf)
     evens = [(i, i + 1) for i in range(0, row_blocks - 1, 2)]
     odds = [(i, i + 1) for i in range(1, row_blocks - 1, 2)]
     even = lax.ppermute(even, "tm", evens + [(j, i) for i, j in evens])
     odd = lax.ppermute(odd, "tm", odds + [(j, i) for i, j in odds])
     bands = band_matrices(psf, width // BLOCK)
-    sent = filter_epochs(main, even, odd, bands, chips)
+    middle = filter_middle(main, bands)
+    sent = filter_border(main, odd, even, middle, bands, chips)
 
     swap = [(i, i ^ 1) for i in range(devices)]
     cols = width // devices

time: 29.8 us -> 28.5 us (0.956)
  the two profiles are of different devices: /device:TPU:5 before, /device:TPU:1 now
where the time goes in v4:
time: 28.5 us; the launch traced here: 28.3 us
  starting transfers between devices  17.6 us (62%)
  Pallas kernels  9.57 us (34%)
  between operations  0.73 us (3%)
  waiting for transfers between devices  0.45 us (2%)
    ppermute x4, starting transfers between devices, on_device(): pieces += [got[k], lax.ppermute(got[k][cols:], 'space', swap)]  8.57 us
    pallas_call x3, Pallas kernels, stack_epochs(): pl.pallas_call(functools.partial(stack_kernel, members, vels, not sums, f...  5.56 us
    ppermute x1, starting transfers between devices, on_device(): even = lax.ppermute(even, 'tm', evens + [(j, i) for i, j in evens])  4.56 us
    ppermute x3, starting transfers between devices, on_device(): got[k] = lax.ppermute(sent[k], 'space', pairs)  3.75 us
    pallas_call x1, Pallas kernels, prepare(): pl.pallas_call(prepare_kernel, out_shape=(jax.ShapeDtypeStruct((2, epochs...  1.26 us
    pallas_call x1, Pallas kernels, filter_middle(): pl.pallas_call(middle_kernel, out_shape=jax.ShapeDtypeStruct((2 * epochs,...  1 us
    pallas_call x1, Pallas kernels, filter_border(): pl.pallas_call(functools.partial(border_kernel, chips), out_shape=(piece,...  0.93 us
    pallas_call x1, Pallas kernels, band_matrices(): pl.pallas_call(band_kernel, out_shape=shapes, in_specs=[VMEM], out_specs=...  0.82 us
  transfers between devices with their start and end apart: 9, of which 2 were waited for; matrix products, arithmetic and copies ran while one was open for 0% of the time, Pallas kernels for 19%

profile of v4, /device:TPU:1, one launch (start us, length us, event | category | flops | bytes accessed | tf_op | source)
XLA Modules:
  0.0 28.3 jit_solution(15907746358250855758)
XLA Ops:
  0.6 1.3 %prepare.1 = (bf16[2,2,128,256]{3,2,1,0:T(8,128)(2,1)S(1)}, bf16[2,2,24,256]{3,2,1,0:T(8,128)(2,1)S(1)}, bf16[2,2,24,256]{3,2,1,0:T(8,128)(2,1)S(1)}, f32[15,15]{1,0:T(8,128)S(1)}) custom-call(f32[2,256,128]{2,1,0:T(8,128)} %image_hbm.1, f32[2,256,128]{2,1,0:T(8,128)} %inv_var_hbm.1, f32[15,15]{1,0:T(8,128)} %psf_hbm.1), custom_call_target="tpu_custom_call" | custom-call | tf_op jit(solution)/shard_map/prepare/pallas_call | solution.py:48
  1.9 0.7 %collective-permute-start = (bf16[2,2,24,256]{3,2,1,0:T(8,128)(2,1)S(1)}, bf16[2,2,24,256]{3,2,1,0:T(8,128)(2,1)S(1)}, u32[]{:S(2)}, u32[]{:S(2)}) collective-permute-start(bf16[2,2,24,256]{3,2,1,0:T(8,128)(2,1)S(1)} %get-tuple-element.13), channel_id=1, source_target_pairs={{8,16},{16,8},{9,17},{17,9},{10,18},{18,10},{11,19},{19,11},{12,20... | collective-permute-start | bytes 147464 | tf_op jit(solution)/shard_map/ppermute | solution.py:379
  2.6 4.6 %collective-permute-start.1 = (bf16[2,2,24,256]{3,2,1,0:T(8,128)(2,1)S(1)}, bf16[2,2,24,256]{3,2,1,0:T(8,128)(2,1)S(1)}, u32[]{:S(2)}, u32[]{:S(2)}) collective-permute-start(bf16[2,2,24,256]{3,2,1,0:T(8,128)(2,1)S(1)} %get-tuple-element.14), channel_id=1, source_target_pairs={{0,8},{16,24},{8,0},{24,16},{1,9},{17,25},{9,1},{25,17},{2,10},{18... | collective-permute-start | bytes 147464 | tf_op jit(solution)/shard_map/ppermute | solution.py:378
  7.1 0.8 %band.1.band_ref = bf16[2,3840,256]{2,1,0:T(8,128)(2,1)S(1)} custom-call(f32[15,15]{1,0:T(8,128)S(1)} %get-tuple-element.15.psf_ref), custom_call_target="tpu_custom_call" | custom-call | tf_op jit(solution)/shard_map/band/pallas_call | solution.py:103
  8.0 0.0 copy-start
  8.0 1.0 %middle.1.middle_ref = f32[4,96,256]{2,1,0:T(8,128)S(1)} custom-call(bf16[2,2,128,256]{3,2,1,0:T(8,128)(2,1)S(1)} %get-tuple-element.12.main_ref, bf16[2,3840,256]{2,1,0:T(8,128)(2,1)S(1)} %band.1.band_ref), custom_call_target="tpu_custom_call" | custom-call | tf_op jit(solution)/shard_map/middle/pallas_call | solution.py:160
  9.0 0.0 collective-permute-done.odd_ref
  9.0 0.1 collective-permute-done.1.even_ref
  9.0 0.9 %border.1 = (bf16[96,640]{1,0:T(8,128)(2,1)S(1)}, bf16[96,640]{1,0:T(8,128)(2,1)S(1)}, bf16[96,640]{1,0:T(8,128)(2,1)S(1)}, bf16[96,640]{1,0:T(8,128)(2,1)S(1)}) custom-call(bf16[2,2,128,256]{3,2,1,0:T(8,128)(2,1)S(1)} %get-tuple-element.12.main_ref, bf16[2,2,24,256]{3,2,1,0:T(8,128)(2,1)S(1)} %collective-permute-done.odd_ref, ...), custom_call_target="tpu_custom_call" | custom-call | tf_op jit(solution)/shard_map/border/pallas_call | solution.py:239
  10.0 3.4 %collective-permute-start.3 = (bf16[96,640]{1,0:T(8,128)(2,1)S(1)}, bf16[96,640]{1,0:T(8,128)(2,1)S(1)}, u32[]{:S(2)}, u32[]{:S(2)}) collective-permute-start(bf16[96,640]{1,0:T(8,128)(2,1)S(1)} %get-tuple-element.17), channel_id=1, source_target_pairs={{0,6},{1,7},{2,4},{3,5},{4,2},{5,3},{6,0},{7,1},{8,14},{9,15},{10,... | collective-permute-start | bytes 368648 | tf_op jit(solution)/shard_map/ppermute | solution.py:390
  13.4 0.0 collective-permute-start.7
  13.4 0.4 %collective-permute-start.2 = (bf16[96,640]{1,0:T(8,128)(2,1)S(1)}, bf16[96,640]{1,0:T(8,128)(2,1)S(1)}, u32[]{:S(2)}, u32[]{:S(2)}) collective-permute-start(bf16[96,640]{1,0:T(8,128)(2,1)S(1)} %get-tuple-element.16), channel_id=1, source_target_pairs={{0,4},{1,5},{2,6},{3,7},{4,0},{5,1},{6,2},{7,3},{8,12},{9,13},{10,... | collective-permute-start | bytes 368648 | tf_op jit(solution)/shard_map/ppermute | solution.py:390
  13.7 2.6 %collective-permute-start.5 = (bf16[64,640]{1,0:T(8,128)(2,1)S(1)}, bf16[64,640]{1,0:T(8,128)(2,1)S(1)}, u32[]{:S(2)}, u32[]{:S(2)}) collective-permute-start(bf16[64,640]{1,0:T(8,128)(2,1)S(1)} %slice.13), channel_id=1, source_target_pairs={{0,1},{1,0},{2,3},{3,2},{4,5},{5,4},{6,7},{7,6},{8,9},{9,8},{10,11... | collective-permute-start | bytes 245768 | tf_op jit(solution)/shard_map/ppermute | solution.py:400
  16.3 0.0 collective-permute-done.3.refs_0_
  16.3 3.2 %collective-permute-start.4 = (bf16[64,640]{1,0:T(8,128)(2,1)S(1)}, bf16[64,640]{1,0:T(8,128)(2,1)S(1)}, u32[]{:S(2)}, u32[]{:S(2)}) collective-permute-start(bf16[64,640]{1,0:T(8,128)(2,1)S(1)} %slice.16), channel_id=1, source_target_pairs={{0,1},{1,0},{2,3},{3,2},{4,5},{5,4},{6,7},{7,6},{8,9},{9,8},{10,11... | collective-permute-start | bytes 245768 | tf_op jit(solution)/shard_map/ppermute | solution.py:400
  19.6 0.0 collective-permute-done.7.refs_0_
  19.6 1.5 %collective-permute-start.8 = (bf16[64,640]{1,0:T(8,128)(2,1)S(1)}, bf16[64,640]{1,0:T(8,128)(2,1)S(1)}, u32[]{:S(2)}, u32[]{:S(2)}) collective-permute-start(bf16[64,640]{1,0:T(8,128)(2,1)S(1)} %slice.17), channel_id=1, source_target_pairs={{0,1},{1,0},{2,3},{3,2},{4,5},{5,4},{6,7},{7,6},{8,9},{9,8},{10,11... | collective-permute-start | bytes 245768 | tf_op jit(solution)/shard_map/ppermute | solution.py:400
  21.1 0.0 collective-permute-done.5.refs_3_
  21.1 0.0 collective-permute-done.4.refs_1_
  21.1 0.0 copy-done
  21.1 2.0 %stack_part.2.refs_2_ = f32[16,2,32,128]{3,2,1,0:T(8,128)S(1)} custom-call(s32[32,16]{1,0:T(8,128)S(1)} %bitcast.3, bf16[96,640]{1,0:T(8,128)(2,1)S(1)} %collective-permute-done.3.refs_0_, bf16[64,640]{1,0:T(8,128)(2,1)S(1)} %collective-permute-done.4.refs_1_, bf16[96,640]{1,0:T(8,128)(2,1)S(1)} %get-tuple-element.18.refs_2_, ...), custom_call_target="tpu_custom_call" | custom-call | tf_op jit(solution)/shard_map/stack_part/pallas_call | solution.py:357
  23.1 0.4 %collective-permute-done.2.refs_0_ = bf16[96,640]{1,0:T(8,128)(2,1)S(1)} collective-permute-done((bf16[96,640]{1,0:T(8,128)(2,1)S(1)}, bf16[96,640]{1,0:T(8,128)(2,1)S(1)}, u32[]{:S(2)}, u32[]{:S(2)}) %collective-permute-start.2) | collective-permute-done | bytes 122912 | tf_op jit(solution)/shard_map/ppermute | solution.py:390
  23.5 1.3 %collective-permute-start.6 = (bf16[64,640]{1,0:T(8,128)(2,1)S(1)}, bf16[64,640]{1,0:T(8,128)(2,1)S(1)}, u32[]{:S(2)}, u32[]{:S(2)}) collective-permute-start(bf16[64,640]{1,0:T(8,128)(2,1)S(1)} %slice.14), channel_id=1, source_target_pairs={{0,1},{1,0},{2,3},{3,2},{4,5},{5,4},{6,7},{7,6},{8,9},{9,8},{10,11... | collective-permute-start | bytes 245768 | tf_op jit(solution)/shard_map/ppermute | solution.py:400
  24.8 0.0 collective-permute-done.8.refs_1_
  24.8 1.5 %stack_part.3.refs_2_ = f32[16,2,32,128]{3,2,1,0:T(8,128)S(1)} custom-call(s32[32,16]{1,0:T(8,128)S(1)} %bitcast.4, bf16[96,640]{1,0:T(8,128)(2,1)S(1)} %collective-permute-done.7.refs_0_, bf16[64,640]{1,0:T(8,128)(2,1)S(1)} %collective-permute-done.8.refs_1_, f32[16,2,32,128]{3,2,1,0:T(8,128)S(1)} %stack_part.2.refs_2_), custom_call_target="tpu_custom_call" | custom-call | tf_op jit(solution)/shard_map/stack_part/pallas_call | solution.py:357
  26.2 0.0 collective-permute-done.6.refs_1_
  26.2 2.1 %stack_end.1 = (f32[32,128]{1,0:T(8,128)}, f32[32,128]{1,0:T(8,128)}) custom-call(s32[32,16]{1,0:T(8,128)S(1)} %bitcast.5, bf16[96,640]{1,0:T(8,128)(2,1)S(1)} %collective-permute-done.2.refs_0_, bf16[64,640]{1,0:T(8,128)(2,1)S(1)} %collective-permute-done.6.refs_1_, f32[16,2,32,128]{3,2,1,0:T(8,128)S(1)} %stack_part.3.refs_2_), custom_call_target="tpu_custom_call" | custom-call | tf_op jit(solution)/shard_map/stack_end/pallas_call | solution.py:357
  (4 shorter events, 0.0 us)
Async XLA Ops:
  1.9 7.1 %collective-permute-start = (bf16[2,2,24,256]{3,2,1,0:T(8,128)(2,1)S(1)}, bf16[2,2,24,256]{3,2,1,0:T(8,128)(2,1)S(1)}, u32[]{:S(2)}, u32[]{:S(2)}) collective-permute-start(bf16[2,2,24,256]{3,2,1,0:T(8,128)(2,1)S(1)} %get-tuple-element.13), channel_id=1, source_target_pairs={{8,16},{16,8},{9,17},{17,9},{10,18},{18,10},{11,19},{19,11},{12,20... | collective-permute-start | bytes 147464 | tf_op jit(solution)/shard_map/ppermute | solution.py:379
  2.6 6.5 %collective-permute-start.1 = (bf16[2,2,24,256]{3,2,1,0:T(8,128)(2,1)S(1)}, bf16[2,2,24,256]{3,2,1,0:T(8,128)(2,1)S(1)}, u32[]{:S(2)}, u32[]{:S(2)}) collective-permute-start(bf16[2,2,24,256]{3,2,1,0:T(8,128)(2,1)S(1)} %get-tuple-element.14), channel_id=1, source_target_pairs={{0,8},{16,24},{8,0},{24,16},{1,9},{17,25},{9,1},{25,17},{2,10},{18... | collective-permute-start | bytes 147464 | tf_op jit(solution)/shard_map/ppermute | solution.py:378
  8.0 13.1 %copy-start = (s32[16,16,2]{1,2,0:T(2,128)S(1)}, s32[16,16,2]{1,2,0:T(2,128)}, u32[]{:S(2)}) copy-start(s32[16,16,2]{1,2,0:T(2,128)} %param.7) | copy-start | bytes 6148
  10.0 6.4 %collective-permute-start.3 = (bf16[96,640]{1,0:T(8,128)(2,1)S(1)}, bf16[96,640]{1,0:T(8,128)(2,1)S(1)}, u32[]{:S(2)}, u32[]{:S(2)}) collective-permute-start(bf16[96,640]{1,0:T(8,128)(2,1)S(1)} %get-tuple-element.17), channel_id=1, source_target_pairs={{0,6},{1,7},{2,4},{3,5},{4,2},{5,3},{6,0},{7,1},{8,14},{9,15},{10,... | collective-permute-start | bytes 368648 | tf_op jit(solution)/shard_map/ppermute | solution.py:390
  13.4 6.2 %collective-permute-start.7 = (bf16[96,640]{1,0:T(8,128)(2,1)S(1)}, bf16[96,640]{1,0:T(8,128)(2,1)S(1)}, u32[]{:S(2)}, u32[]{:S(2)}) collective-permute-start(bf16[96,640]{1,0:T(8,128)(2,1)S(1)} %get-tuple-element.20), channel_id=1, source_target_pairs={{0,2},{1,3},{2,0},{3,1},{4,6},{5,7},{6,4},{7,5},{8,10},{9,11},{10,... | collective-permute-start | bytes 368648 | tf_op jit(solution)/shard_map/ppermute | solution.py:390
  13.4 10.1 %collective-permute-start.2 = (bf16[96,640]{1,0:T(8,128)(2,1)S(1)}, bf16[96,640]{1,0:T(8,128)(2,1)S(1)}, u32[]{:S(2)}, u32[]{:S(2)}) collective-permute-start(bf16[96,640]{1,0:T(8,128)(2,1)S(1)} %get-tuple-element.16), channel_id=1, source_target_pairs={{0,4},{1,5},{2,6},{3,7},{4,0},{5,1},{6,2},{7,3},{8,12},{9,13},{10,... | collective-permute-start | bytes 368648 | tf_op jit(solution)/shard_map/ppermute | solution.py:390
  13.7 7.4 %collective-permute-start.5 = (bf16[64,640]{1,0:T(8,128)(2,1)S(1)}, bf16[64,640]{1,0:T(8,128)(2,1)S(1)}, u32[]{:S(2)}, u32[]{:S(2)}) collective-permute-start(bf16[64,640]{1,0:T(8,128)(2,1)S(1)} %slice.13), channel_id=1, source_target_pairs={{0,1},{1,0},{2,3},{3,2},{4,5},{5,4},{6,7},{7,6},{8,9},{9,8},{10,11... | collective-permute-start | bytes 245768 | tf_op jit(solution)/shard_map/ppermute | solution.py:400
  16.3 4.8 %collective-permute-start.4 = (bf16[64,640]{1,0:T(8,128)(2,1)S(1)}, bf16[64,640]{1,0:T(8,128)(2,1)S(1)}, u32[]{:S(2)}, u32[]{:S(2)}) collective-permute-start(bf16[64,640]{1,0:T(8,128)(2,1)S(1)} %slice.16), channel_id=1, source_target_pairs={{0,1},{1,0},{2,3},{3,2},{4,5},{5,4},{6,7},{7,6},{8,9},{9,8},{10,11... | collective-permute-start | bytes 245768 | tf_op jit(solution)/shard_map/ppermute | solution.py:400
  19.6 5.2 %collective-permute-start.8 = (bf16[64,640]{1,0:T(8,128)(2,1)S(1)}, bf16[64,640]{1,0:T(8,128)(2,1)S(1)}, u32[]{:S(2)}, u32[]{:S(2)}) collective-permute-start(bf16[64,640]{1,0:T(8,128)(2,1)S(1)} %slice.17), channel_id=1, source_target_pairs={{0,1},{1,0},{2,3},{3,2},{4,5},{5,4},{6,7},{7,6},{8,9},{9,8},{10,11... | collective-permute-start | bytes 245768 | tf_op jit(solution)/shard_map/ppermute | solution.py:400
  23.5 2.7 %collective-permute-start.6 = (bf16[64,640]{1,0:T(8,128)(2,1)S(1)}, bf16[64,640]{1,0:T(8,128)(2,1)S(1)}, u32[]{:S(2)}, u32[]{:S(2)}) collective-permute-start(bf16[64,640]{1,0:T(8,128)(2,1)S(1)} %slice.14), channel_id=1, source_target_pairs={{0,1},{1,0},{2,3},{3,2},{4,5},{5,4},{6,7},{7,6},{8,9},{9,8},{10,11... | collective-permute-start | bytes 245768 | tf_op jit(solution)/shard_map/ppermute | solution.py:400

commit v5 on v4

--- a/solution.py
+++ b/solution.py
@@ -253,13 +253,11 @@
     )(main, odd, even, middle, *bands)
 
 
-def stack_kernel(members, vels, first, final, shifts_hbm, *refs):
-    count = 2 * len(members)
-    scratch = 5 if final else 3
+def stack_kernel(slots, vels, first, final, shifts_ref, *refs):
+    count = len(slots)
+    scratch = 4 if final else 2
     pieces, refs, scratch = refs[:count], refs[count:-scratch], refs[-scratch:]
-    frames, shifts_ref, sems = scratch[:3]
-    table = pltpu.make_async_copy(shifts_hbm, shifts_ref, sems.at[0])
-    table.start()
+    frames, sems = scratch[:2]
     if not first:
         start_ref, refs = refs[0], refs[1:]
     place = lax.axis_index("space")
@@ -268,24 +266,25 @@
     window = cols + 2 * MAXSHIFT
     parts = pieces[0].shape[1] // LANES
     epochs = (parts - 1) // 2
-    for slot in range(count):
+    for slot, (_, flip) in enumerate(slots):
         for half in range(2):
             own = 2 * cols * core if half == 0 else cols * (1 - core)
-            start = pl.multiple_of(own, cols) if slot % 2 == 0 else half * cols
+            start = pl.multiple_of(own, cols) if flip == 0 else half * cols
             for part in range(parts):
                 base = (slot * parts + part) * window + half * cols
                 frames[base : base + cols] = pieces[slot][
                     pl.ds(start, cols), part * LANES : (part + 1) * LANES
                 ].astype(F32)
-    table.wait()
+    total_epochs = shifts_ref.shape[0] // vels
     lane = lax.broadcasted_iota(jnp.int32, (cols, LANES), 1)
 
     def add_slot(slot, k, flip, v, upper, lower):
         owner = 2 * jnp.bitwise_xor(chip, k) + jnp.bitwise_xor(core, flip)
         for ep in range(epochs):
             epoch = owner * epochs + ep
-            right = MAXSHIFT + shifts_ref[2 * v, epoch]
-            down = MAXSHIFT + shifts_ref[2 * v + 1, epoch]
+            both = shifts_ref[pl.ds(v * total_epochs + epoch, 1), :][0, 0]
+            right = lax.shift_right_logical(both, 6)
+            down = jnp.bitwise_and(both, 63)
             base = slot * (parts * window) + right
             extra = frames[pl.ds(base + 2 * epochs * window, cols), :]
             sums = []
@@ -304,12 +303,11 @@
             sums = (jnp.zeros((cols, LANES), F32), jnp.zeros((cols, LANES), F32))
         else:
             sums = (start_ref[v, 0], start_ref[v, 1])
-        for i, k in enumerate(members):
-            for flip in range(2):
-                sums = add_slot(2 * i + flip, k, flip, v, *sums)
+        for slot, (k, flip) in enumerate(slots):
+            sums = add_slot(slot, k, flip, v, *sums)
         return sums
 
-    unroll = vels if len(members) <= 4 else 1
+    unroll = vels if count <= 8 else 1
     if final:
         best_ref, score_ref = refs
 
@@ -321,12 +319,12 @@
 
         top = jnp.full((cols, LANES), -jnp.inf, F32)
         top, total = lax.fori_loop(0, vels, visit, (top, jnp.zeros((cols, LANES), F32)), unroll=unroll)
-        best, score = scratch[3:]
+        best, score = scratch[2:]
         best[...] = top
-        best_copy = pltpu.make_async_copy(best, best_ref, sems.at[1])
+        best_copy = pltpu.make_async_copy(best, best_ref, sems.at[0])
         best_copy.start()
         score[...] = jnp.log(total / vels)
-        score_copy = pltpu.make_async_copy(score, score_ref, sems.at[2])
+        score_copy = pltpu.make_async_copy(score, score_ref, sems.at[1])
         score_copy.start()
         best_copy.wait()
         score_copy.wait()
@@ -340,8 +338,7 @@
         lax.fori_loop(0, vels, keep, 0, unroll=unroll)
 
 
-def stack_epochs(shifts, members, pieces, sums, final, cols, rows):
-    vels = shifts.shape[0] // 2
+def stack_epochs(shifts, vels, slots, pieces, sums, final, cols, rows):
     parts = pieces[0].shape[1] // LANES
     if final:
         out_shape = (jax.ShapeDtypeStruct((cols, rows), F32),) * 2
@@ -349,15 +346,14 @@
         out_shape = (jax.ShapeDtypeStruct((vels, 2, cols, rows), F32),)
     scratch = [
         pltpu.VMEM((len(pieces) * parts * (cols + 2 * MAXSHIFT), LANES), F32),
-        pltpu.SMEM(shifts.shape, jnp.int32),
-        pltpu.SemaphoreType.DMA((3,)),
+        pltpu.SemaphoreType.DMA((2,)),
     ]
     if final:
         scratch += [pltpu.VMEM((cols, rows), F32)] * 2
     return pl.pallas_call(
-        functools.partial(stack_kernel, members, vels, not sums, final),
+        functools.partial(stack_kernel, slots, vels, not sums, final),
         out_shape=out_shape,
-        in_specs=[ANY] + [VMEM] * (len(pieces) + len(sums)),
+        in_specs=[VMEM] * (1 + len(pieces) + len(sums)),
         out_specs=[ANY if final else VMEM] * len(out_shape),
         scratch_shapes=scratch,
         compiler_params=PARAMS,
@@ -370,7 +366,7 @@
     devices = lax.axis_size("space")
     row_blocks = lax.axis_size("tm")
     chips = devices // 2
-    table = jnp.transpose(shifts, (0, 2, 1)).reshape(2 * shifts.shape[0], shifts.shape[1])
+    table = jnp.sum((shifts + MAXSHIFT) * jnp.array([64, 1], jnp.int32), axis=2).reshape(-1, 1)
 
     main, even, odd, psf = prepare(image, inv_var, psf)
     evens = [(i, i + 1) for i in range(0, row_blocks - 1, 2)]
@@ -388,18 +384,17 @@
     for k in range(1, chips):
         pairs = [(2 * i + c, 2 * (i ^ k) + c) for i in range(chips) for c in range(2)]
         got[k] = lax.ppermute(sent[k], "space", pairs)
+    def stack(slots, sums, final):
+        pieces = []
+        for k, flip in slots:
+            pieces.append(lax.ppermute(got[k][cols:], "space", swap) if flip else got[k])
+        return stack_epochs(table, shifts.shape[0], slots, pieces, sums, final, cols, rows)
+
     last = chips // 2
-    first = tuple(k for k in reversed(range(chips)) if k not in (1, last))
-    steps = (first, (1,), (last,)) if last > 1 else (first, (last,))
-    sums = ()
-    for step, members in enumerate(steps):
-        if step == 1:
-            got[last], sums = lax.optimization_barrier((got[last], sums))
-        pieces = []
-        for k in members:
-            pieces += [got[k], lax.ppermute(got[k][cols:], "space", swap)]
-        sums = stack_epochs(table, members, pieces, sums, members == (last,), cols, rows)
-    return sums
+    sums = stack([(k, flip) for k in reversed(range(chips)) if k != last for flip in range(2)], (), False)
+    got[last], sums = lax.optimization_barrier((got[last], sums))
+    sums = stack([(last, 0)], sums, False)
+    return stack([(last, 1)], sums, True)
 
 
 def solution(mesh):

time: 28.5 us -> 27.2 us (0.954)
  the two profiles are of different devices: /device:TPU:1 before, /device:TPU:0 now
where the time goes in v5:
time: 27.2 us; the launch traced here: 27.1 us
  starting transfers between devices  11.1 us (41%)
  waiting for transfers between devices  7.52 us (28%)
  Pallas kernels  7.36 us (27%)
  between operations  0.8 us (3%)
    ppermute x1, starting transfers between devices, on_device(): even = lax.ppermute(even, 'tm', evens + [(j, i) for i, j in evens])  5.74 us
    ppermute x3, waiting for transfers between devices, on_device(): got[k] = lax.ppermute(sent[k], 'space', pairs)  5.02 us
    ppermute x3, starting transfers between devices, on_device(): got[k] = lax.ppermute(sent[k], 'space', pairs)  4.45 us
    pallas_call x3, Pallas kernels, stack_epochs(): pl.pallas_call(functools.partial(stack_kernel, slots, vels, not sums, fin...  3.35 us
    ppermute x4, waiting for transfers between devices, stack(): lax.ppermute(got[k][cols:], 'space', swap)  1.87 us
    pallas_call x1, Pallas kernels, prepare(): pl.pallas_call(prepare_kernel, out_shape=(jax.ShapeDtypeStruct((2, epochs...  1.26 us
    pallas_call x1, Pallas kernels, filter_middle(): pl.pallas_call(middle_kernel, out_shape=jax.ShapeDtypeStruct((2 * epochs,...  1 us
    pallas_call x1, Pallas kernels, filter_border(): pl.pallas_call(functools.partial(border_kernel, chips), out_shape=(piece,...  0.92 us
  transfers between devices with their start and end apart: 9, of which 6 were waited for; matrix products, arithmetic and copies ran while one was open for 1% of the time, Pallas kernels for 15%

profile of v5, /device:TPU:0, one launch (start us, length us, event | category | flops | bytes accessed | tf_op | source)
XLA Modules:
  0.0 27.1 jit_solution(14338338860743325223)
XLA Ops:
  0.6 1.3 %prepare.1 = (bf16[2,2,128,256]{3,2,1,0:T(8,128)(2,1)S(1)}, bf16[2,2,24,256]{3,2,1,0:T(8,128)(2,1)S(1)}, bf16[2,2,24,256]{3,2,1,0:T(8,128)(2,1)S(1)}, f32[15,15]{1,0:T(8,128)S(1)}) custom-call(f32[2,256,128]{2,1,0:T(8,128)} %image_hbm.1, f32[2,256,128]{2,1,0:T(8,128)} %inv_var_hbm.1, f32[15,15]{1,0:T(8,128)} %psf_hbm.1), custom_call_target="tpu_custom_call" | custom-call | tf_op jit(solution)/shard_map/prepare/pallas_call | solution.py:48
  1.9 0.7 %collective-permute-start = (bf16[2,2,24,256]{3,2,1,0:T(8,128)(2,1)S(1)}, bf16[2,2,24,256]{3,2,1,0:T(8,128)(2,1)S(1)}, u32[]{:S(2)}, u32[]{:S(2)}) collective-permute-start(bf16[2,2,24,256]{3,2,1,0:T(8,128)(2,1)S(1)} %get-tuple-element.13), channel_id=1, source_target_pairs={{8,16},{16,8},{9,17},{17,9},{10,18},{18,10},{11,19},{19,11},{12,20... | collective-permute-start | bytes 147464 | tf_op jit(solution)/shard_map/ppermute | solution.py:375
  2.6 5.7 %collective-permute-start.1 = (bf16[2,2,24,256]{3,2,1,0:T(8,128)(2,1)S(1)}, bf16[2,2,24,256]{3,2,1,0:T(8,128)(2,1)S(1)}, u32[]{:S(2)}, u32[]{:S(2)}) collective-permute-start(bf16[2,2,24,256]{3,2,1,0:T(8,128)(2,1)S(1)} %get-tuple-element.14), channel_id=1, source_target_pairs={{0,8},{16,24},{8,0},{24,16},{1,9},{17,25},{9,1},{25,17},{2,10},{18... | collective-permute-start | bytes 147464 | tf_op jit(solution)/shard_map/ppermute | solution.py:374
  8.3 0.8 %band.1.band_ref = bf16[2,3840,256]{2,1,0:T(8,128)(2,1)S(1)} custom-call(f32[15,15]{1,0:T(8,128)S(1)} %get-tuple-element.15.psf_ref), custom_call_target="tpu_custom_call" | custom-call | tf_op jit(solution)/shard_map/band/pallas_call | solution.py:103
  9.1 0.0 copy-start
  9.1 0.0 copy-start.1
  9.2 1.0 %middle.1.middle_ref = f32[4,96,256]{2,1,0:T(8,128)S(1)} custom-call(bf16[2,2,128,256]{3,2,1,0:T(8,128)(2,1)S(1)} %get-tuple-element.12.main_ref, bf16[2,3840,256]{2,1,0:T(8,128)(2,1)S(1)} %band.1.band_ref), custom_call_target="tpu_custom_call" | custom-call | tf_op jit(solution)/shard_map/middle/pallas_call | solution.py:160
  10.2 0.0 collective-permute-done.odd_ref
  10.2 0.6 %collective-permute-done.1.even_ref = bf16[2,2,24,256]{3,2,1,0:T(8,128)(2,1)S(1)} collective-permute-done((bf16[2,2,24,256]{3,2,1,0:T(8,128)(2,1)S(1)}, bf16[2,2,24,256]{3,2,1,0:T(8,128)(2,1)S(1)}, u32[]{:S(2)}, u32[]{:S(2)}) %collective-permute-start.1) | collective-permute-done | bytes 49184 | tf_op jit(solution)/shard_map/ppermute | solution.py:374
  10.8 0.9 %border.1 = (bf16[96,640]{1,0:T(8,128)(2,1)S(1)}, bf16[96,640]{1,0:T(8,128)(2,1)S(1)}, bf16[96,640]{1,0:T(8,128)(2,1)S(1)}, bf16[96,640]{1,0:T(8,128)(2,1)S(1)}) custom-call(bf16[2,2,128,256]{3,2,1,0:T(8,128)(2,1)S(1)} %get-tuple-element.12.main_ref, bf16[2,2,24,256]{3,2,1,0:T(8,128)(2,1)S(1)} %collective-permute-done.odd_ref, ...), custom_call_target="tpu_custom_call" | custom-call | tf_op jit(solution)/shard_map/border/pallas_call | solution.py:239
  11.7 3.7 %collective-permute-start.3 = (bf16[96,640]{1,0:T(8,128)(2,1)S(1)}, bf16[96,640]{1,0:T(8,128)(2,1)S(1)}, u32[]{:S(2)}, u32[]{:S(2)}) collective-permute-start(bf16[96,640]{1,0:T(8,128)(2,1)S(1)} %get-tuple-element.17), channel_id=1, source_target_pairs={{0,6},{1,7},{2,4},{3,5},{4,2},{5,3},{6,0},{7,1},{8,14},{9,15},{10,... | collective-permute-start | bytes 368648 | tf_op jit(solution)/shard_map/ppermute | solution.py:386
  15.4 0.0 collective-permute-start.5
  15.4 0.8 %collective-permute-start.2 = (bf16[96,640]{1,0:T(8,128)(2,1)S(1)}, bf16[96,640]{1,0:T(8,128)(2,1)S(1)}, u32[]{:S(2)}, u32[]{:S(2)}) collective-permute-start(bf16[96,640]{1,0:T(8,128)(2,1)S(1)} %get-tuple-element.16), channel_id=1, source_target_pairs={{0,4},{1,5},{2,6},{3,7},{4,0},{5,1},{6,2},{7,3},{8,12},{9,13},{10,... | collective-permute-start | bytes 368648 | tf_op jit(solution)/shard_map/ppermute | solution.py:386
  16.2 0.1 collective-permute-start.7
  16.3 3.2 %collective-permute-done.3.refs_0_ = bf16[96,640]{1,0:T(8,128)(2,1)S(1)} collective-permute-done((bf16[96,640]{1,0:T(8,128)(2,1)S(1)}, bf16[96,640]{1,0:T(8,128)(2,1)S(1)}, u32[]{:S(2)}, u32[]{:S(2)}) %collective-permute-start.3) | collective-permute-done | bytes 122912 | tf_op jit(solution)/shard_map/ppermute | solution.py:386
  19.5 0.1 collective-permute-start.4
  19.5 1.4 %collective-permute-done.5.refs_2_ = bf16[96,640]{1,0:T(8,128)(2,1)S(1)} collective-permute-done((bf16[96,640]{1,0:T(8,128)(2,1)S(1)}, bf16[96,640]{1,0:T(8,128)(2,1)S(1)}, u32[]{:S(2)}, u32[]{:S(2)}) %collective-permute-start.5) | collective-permute-done | bytes 122912 | tf_op jit(solution)/shard_map/ppermute | solution.py:386
  21.0 0.1 collective-permute-start.6
  21.0 0.0 copy-done
  21.1 0.0 copy-done.1
  21.1 0.1 multiply_reduce_fusion
  21.2 0.1 reshape.9.shifts_ref
  21.3 0.0 collective-permute-done.7.refs_5_
  21.3 0.0 collective-permute-done.4.refs_1_
  21.3 1.0 %collective-permute-done.6.refs_3_ = bf16[64,640]{1,0:T(8,128)(2,1)S(1)} collective-permute-done((bf16[64,640]{1,0:T(8,128)(2,1)S(1)}, bf16[64,640]{1,0:T(8,128)(2,1)S(1)}, u32[]{:S(2)}, u32[]{:S(2)}) %collective-permute-start.6) | collective-permute-done | bytes 81952 | tf_op jit(solution)/shard_map/ppermute | solution.py:390
  22.3 1.9 %stack_part.2.refs_1_ = f32[16,2,32,128]{3,2,1,0:T(8,128)S(1)} custom-call(s32[256,1]{1,0:T(8,128)S(1)} %reshape.9.shifts_ref, bf16[96,640]{1,0:T(8,128)(2,1)S(1)} %collective-permute-done.3.refs_0_, bf16[64,640]{1,0:T(8,128)(2,1)S(1)} %collective-permute-done.4.refs_1_, bf16[96,640]{1,0:T(8,128)(2,1)S(1)} %collective-permute-done.5.refs_2_, ...), custom_call_target="tpu_custom_call" | custom-call | tf_op jit(solution)/shard_map/stack_part/pallas_call | solution.py:353
  24.2 0.4 %collective-permute-done.2.refs_0_ = bf16[96,640]{1,0:T(8,128)(2,1)S(1)} collective-permute-done((bf16[96,640]{1,0:T(8,128)(2,1)S(1)}, bf16[96,640]{1,0:T(8,128)(2,1)S(1)}, u32[]{:S(2)}, u32[]{:S(2)}) %collective-permute-start.2) | collective-permute-done | bytes 122912 | tf_op jit(solution)/shard_map/ppermute | solution.py:386
  24.6 0.1 collective-permute-start.8
  24.7 0.4 %stack_part.3.refs_1_ = f32[16,2,32,128]{3,2,1,0:T(8,128)S(1)} custom-call(s32[256,1]{1,0:T(8,128)S(1)} %reshape.9.shifts_ref, bf16[96,640]{1,0:T(8,128)(2,1)S(1)} %collective-permute-done.2.refs_0_, f32[16,2,32,128]{3,2,1,0:T(8,128)S(1)} %stack_part.2.refs_1_), custom_call_target="tpu_custom_call" | custom-call | tf_op jit(solution)/shard_map/stack_part/pallas_call | solution.py:353
  25.1 0.8 %collective-permute-done.8.refs_0_ = bf16[64,640]{1,0:T(8,128)(2,1)S(1)} collective-permute-done((bf16[64,640]{1,0:T(8,128)(2,1)S(1)}, bf16[64,640]{1,0:T(8,128)(2,1)S(1)}, u32[]{:S(2)}, u32[]{:S(2)}) %collective-permute-start.8) | collective-permute-done | bytes 81952 | tf_op jit(solution)/shard_map/ppermute | solution.py:390
  26.0 1.1 %stack_end.1 = (f32[32,128]{1,0:T(8,128)}, f32[32,128]{1,0:T(8,128)}) custom-call(s32[256,1]{1,0:T(8,128)S(1)} %reshape.9.shifts_ref, bf16[64,640]{1,0:T(8,128)(2,1)S(1)} %collective-permute-done.8.refs_0_, f32[16,2,32,128]{3,2,1,0:T(8,128)S(1)} %stack_part.3.refs_1_), custom_call_target="tpu_custom_call" | custom-call | tf_op jit(solution)/shard_map/stack_end/pallas_call | solution.py:353
  (4 shorter events, 0.0 us)
Async XLA Ops:
  1.9 8.3 %collective-permute-start = (bf16[2,2,24,256]{3,2,1,0:T(8,128)(2,1)S(1)}, bf16[2,2,24,256]{3,2,1,0:T(8,128)(2,1)S(1)}, u32[]{:S(2)}, u32[]{:S(2)}) collective-permute-start(bf16[2,2,24,256]{3,2,1,0:T(8,128)(2,1)S(1)} %get-tuple-element.13), channel_id=1, source_target_pairs={{8,16},{16,8},{9,17},{17,9},{10,18},{18,10},{11,19},{19,11},{12,20... | collective-permute-start | bytes 147464 | tf_op jit(solution)/shard_map/ppermute | solution.py:375
  2.6 8.2 %collective-permute-start.1 = (bf16[2,2,24,256]{3,2,1,0:T(8,128)(2,1)S(1)}, bf16[2,2,24,256]{3,2,1,0:T(8,128)(2,1)S(1)}, u32[]{:S(2)}, u32[]{:S(2)}) collective-permute-start(bf16[2,2,24,256]{3,2,1,0:T(8,128)(2,1)S(1)} %get-tuple-element.14), channel_id=1, source_target_pairs={{0,8},{16,24},{8,0},{24,16},{1,9},{17,25},{9,1},{25,17},{2,10},{18... | collective-permute-start | bytes 147464 | tf_op jit(solution)/shard_map/ppermute | solution.py:374
  9.1 11.9 %copy-start = (s32[16,16,2]{1,2,0:T(2,128)S(1)}, s32[16,16,2]{1,2,0:T(2,128)}, u32[]{:S(2)}) copy-start(s32[16,16,2]{1,2,0:T(2,128)} %param.8) | copy-start | bytes 6148
  9.1 11.9 %copy-start.1 = (s32[2]{0:T(128)S(1)}, s32[2]{0:T(128)}, u32[]{:S(2)}) copy-start(s32[2]{0:T(128)} %constant.6.clone) | copy-start | bytes 28
  11.7 7.7 %collective-permute-start.3 = (bf16[96,640]{1,0:T(8,128)(2,1)S(1)}, bf16[96,640]{1,0:T(8,128)(2,1)S(1)}, u32[]{:S(2)}, u32[]{:S(2)}) collective-permute-start(bf16[96,640]{1,0:T(8,128)(2,1)S(1)} %get-tuple-element.17), channel_id=1, source_target_pairs={{0,6},{1,7},{2,4},{3,5},{4,2},{5,3},{6,0},{7,1},{8,14},{9,15},{10,... | collective-permute-start | bytes 368648 | tf_op jit(solution)/shard_map/ppermute | solution.py:386
  15.4 5.5 %collective-permute-start.5 = (bf16[96,640]{1,0:T(8,128)(2,1)S(1)}, bf16[96,640]{1,0:T(8,128)(2,1)S(1)}, u32[]{:S(2)}, u32[]{:S(2)}) collective-permute-start(bf16[96,640]{1,0:T(8,128)(2,1)S(1)} %get-tuple-element.18), channel_id=1, source_target_pairs={{0,2},{1,3},{2,0},{3,1},{4,6},{5,7},{6,4},{7,5},{8,10},{9,11},{10,... | collective-permute-start | bytes 368648 | tf_op jit(solution)/shard_map/ppermute | solution.py:386
  15.4 9.2 %collective-permute-start.2 = (bf16[96,640]{1,0:T(8,128)(2,1)S(1)}, bf16[96,640]{1,0:T(8,128)(2,1)S(1)}, u32[]{:S(2)}, u32[]{:S(2)}) collective-permute-start(bf16[96,640]{1,0:T(8,128)(2,1)S(1)} %get-tuple-element.16), channel_id=1, source_target_pairs={{0,4},{1,5},{2,6},{3,7},{4,0},{5,1},{6,2},{7,3},{8,12},{9,13},{10,... | collective-permute-start | bytes 368648 | tf_op jit(solution)/shard_map/ppermute | solution.py:386
  16.2 5.1 %collective-permute-start.7 = (bf16[64,640]{1,0:T(8,128)(2,1)S(1)}, bf16[64,640]{1,0:T(8,128)(2,1)S(1)}, u32[]{:S(2)}, u32[]{:S(2)}) collective-permute-start(bf16[64,640]{1,0:T(8,128)(2,1)S(1)} %slice.14), channel_id=1, source_target_pairs={{0,1},{1,0},{2,3},{3,2},{4,5},{5,4},{6,7},{7,6},{8,9},{9,8},{10,11... | collective-permute-start | bytes 245768 | tf_op jit(solution)/shard_map/ppermute | solution.py:390
  19.5 1.8 %collective-permute-start.4 = (bf16[64,640]{1,0:T(8,128)(2,1)S(1)}, bf16[64,640]{1,0:T(8,128)(2,1)S(1)}, u32[]{:S(2)}, u32[]{:S(2)}) collective-permute-start(bf16[64,640]{1,0:T(8,128)(2,1)S(1)} %slice.16), channel_id=1, source_target_pairs={{0,1},{1,0},{2,3},{3,2},{4,5},{5,4},{6,7},{7,6},{8,9},{9,8},{10,11... | collective-permute-start | bytes 245768 | tf_op jit(solution)/shard_map/ppermute | solution.py:390
  21.0 1.3 %collective-permute-start.6 = (bf16[64,640]{1,0:T(8,128)(2,1)S(1)}, bf16[64,640]{1,0:T(8,128)(2,1)S(1)}, u32[]{:S(2)}, u32[]{:S(2)}) collective-permute-start(bf16[64,640]{1,0:T(8,128)(2,1)S(1)} %slice.17), channel_id=1, source_target_pairs={{0,1},{1,0},{2,3},{3,2},{4,5},{5,4},{6,7},{7,6},{8,9},{9,8},{10,11... | collective-permute-start | bytes 245768 | tf_op jit(solution)/shard_map/ppermute | solution.py:390
  24.6 1.3 %collective-permute-start.8 = (bf16[64,640]{1,0:T(8,128)(2,1)S(1)}, bf16[64,640]{1,0:T(8,128)(2,1)S(1)}, u32[]{:S(2)}, u32[]{:S(2)}) collective-permute-start(bf16[64,640]{1,0:T(8,128)(2,1)S(1)} %slice.15), channel_id=1, source_target_pairs={{0,1},{1,0},{2,3},{3,2},{4,5},{5,4},{6,7},{7,6},{8,9},{9,8},{10,11... | collective-permute-start | bytes 245768 | tf_op jit(solution)/shard_map/ppermute | solution.py:390
